TPU v7x, 32 devices: a whole 2x2x4 slice. The times are simulated.
32 devices in a mesh: view: 8 (over z, x), img: 4 (over y, core).
Axes of the slice: x: 2, y: 2, z: 4, core: 2. Of those that a mesh axis runs over, the one named last changes fastest.
Arguments:
- volume: bfloat16 [128, 128, 2048], P('view', 'img'), may hold values from -6 to 6
- occupied: int32 [8, 4, 16], P('view', 'img'), may hold values from -1 to 15, as said below
- sample_counts: int32 [8, 4, 16], P('view', 'img'), may hold values from 6 to 24, as said below
- depth_order: int32 [8], replicated, may hold values from 0 to 7, each once
- colors: bfloat16 [3, 128], replicated, may hold values from 0.049804688 to 1
- density: bfloat16 [128], replicated, may hold values from 0.0019989014 to 0.039794922
Outputs:
- frame: float32 [4, 128, 2048], P(None, 'img', 'view')
Inputs may be any that keep to these rules, and one draw needn't show every extreme that they name: `occupied`: each brick's list names distinct tiles of 0..15 first and then holds -1; a brick lists 16, half, a quarter or an eighth of its tiles (at least 2), and some brick lists all of them. `sample_counts`: every brick has a tile with 24 samples. `depth_order`: A permutation of the bricks along view.
All inputs are finite; a program needn't handle non-finite values.
Results may differ from a plain program's by a relative error of at most 0.0003.
Values may be sent and summed in bfloat16 or wider, within the bound.
A program may use at most 64 MiB of HBM per device.

v0:
```python
import functools
import math

import jax
import jax.numpy as jnp
from jax import lax
from jax.experimental import pallas as pl
from jax.experimental.pallas import tpu as pltpu
from jax.sharding import PartitionSpec as P

LANES = 128
GROUP = 8
PAD = 8
STRIP = 8
LIMIT = 32767
LEVELS = (4096.0, 4096.0, 4096.0, 65536.0)
SPAN_BITS = 13
SPAN = 1 << SPAN_BITS
CHUNK = 16
GRANT = 16 * 2**20


LANE_GATHER = lax.GatherDimensionNumbers(
    offset_dims=(),
    collapsed_slice_dims=(1,),
    start_index_map=(1,),
    operand_batching_dims=(0,),
    start_indices_batching_dims=(0,),
)


def gather_lanes(row, index):
    return lax.gather(
        row, index[..., None], LANE_GATHER, (1, 1), mode=lax.GatherScatterMode.PROMISE_IN_BOUNDS
    )


def rounded(value):
    return value.astype(jnp.bfloat16).astype(jnp.float32)


def prepare_tile(tile, vol, nxt, low, high, vals, grads):
    slices, rows, columns = vol.shape
    last = columns // LANES - 1
    starts = [
        pl.multiple_of(jnp.maximum(tile - 1, 0) * LANES, LANES),
        pl.multiple_of(tile * LANES, LANES),
        pl.multiple_of(jnp.minimum(tile + 1, last) * LANES, LANES),
    ]
    source = lax.broadcasted_iota(jnp.int32, (3 * LANES, LANES), 0) - LANES
    target = lax.broadcasted_iota(jnp.int32, (3 * LANES, LANES), 1)
    inside = jnp.logical_and(
        jnp.logical_or(source >= 0, tile > 0), jnp.logical_or(source < LANES, tile < last)
    )
    sign = jnp.where(source == target + 1, 0.5, jnp.where(source == target - 1, -0.5, 0.0))
    weights = jnp.where(inside, sign, 0.0).astype(jnp.bfloat16)
    here = pl.ds(starts[1], LANES)

    def fill(first, count, ref, at):
        blocks = [
            ref[at : at + count, :, pl.ds(start, LANES)].reshape(count * rows, LANES)
            for start in starts
        ]
        along = jnp.dot(
            jnp.concatenate(blocks, axis=1), weights, preferred_element_type=jnp.float32
        ).reshape(count, rows, LANES)
        mid = blocks[1].astype(jnp.float32).reshape(count, rows, LANES)
        for j in range(count):
            z = first + j
            vals[z, PAD : PAD + rows, :] = mid[j] * 0.5
            vals[z, PAD - 1 : PAD, :] = low[z, :, here] * 0.5
            vals[z, PAD + rows : PAD + rows + 1, :] = high[z, :, here] * 0.5
        for j in range(count):
            z = first + j
            across = vals[z, PAD + 1 : PAD + 1 + rows, :] - vals[z, PAD - 1 : PAD - 1 + rows, :]
            grads[z] = (across * across + along[j] * along[j]) * (1.0 / 0.6) + (1.0 / 0.6)

    for first in range(0, slices, CHUNK):
        fill(first, CHUNK, vol, first)
    fill(slices, 1, nxt, 0)


def packed_table(colors, density):
    entries = [colors[c : c + 1, :] for c in range(3)] + [density]
    lane = lax.broadcasted_iota(jnp.int32, (STRIP, LANES), 1)
    pairs = []
    for entry, level in zip(entries, LEVELS):
        whole = (jnp.broadcast_to(entry, (STRIP, LANES)) * level).astype(jnp.int32)
        after = jnp.where(lane == LANES - 1, 0, pltpu.roll(whole, LANES - 1, 1))
        pairs.append(whole * SPAN + after)
    return pairs


def march_tile(samples, pairs, vals, grads, slices, rows, bins):
    inverse = 1.0 / jnp.full((STRIP, LANES), samples.astype(jnp.float32))
    extinct = (-slices * math.log2(math.e) / LEVELS[3]) * inverse
    half = 0.5 * (bins - 1)
    strips = rows // STRIP

    def group(begin, size, carry):
        carry = list(carry)
        for inner in range(size):
            k = begin + inner
            valid = k < samples
            travel = jnp.minimum(k + 1, samples) * slices
            base = jnp.minimum(lax.div(travel, samples), slices - 1)
            part = (travel - base * samples).astype(jnp.float32) * inverse
            rate = jnp.where(valid, 1.0, 0.0) * extinct
            for strip in range(strips):
                red, green, blue, remain = carry[4 * strip : 4 * strip + 4]
                v0 = vals[base, pl.ds(PAD + strip * STRIP, STRIP), :]
                v1 = vals[base + 1, pl.ds(PAD + strip * STRIP, STRIP), :]
                q0 = grads[base, pl.ds(strip * STRIP, STRIP), :]
                q1 = grads[base + 1, pl.ds(strip * STRIP, STRIP), :]
                level = half * jnp.tanh(v0 + part * (v1 - v0)) + half
                shift = q0 + part * (q1 - q0)
                index = level.astype(jnp.int32)
                frac = level - index.astype(jnp.float32)
                upper = rounded(frac)
                lower = rounded(1.0 - frac)
                both = [gather_lanes(pair, index) for pair in pairs]
                found = [lax.shift_right_logical(p, SPAN_BITS).astype(jnp.float32) for p in both]
                found += [lax.bitwise_and(p, SPAN - 1).astype(jnp.float32) for p in both]
                sigma = lower * found[3] + upper * found[7]
                left = remain * jnp.exp2(sigma * rate)
                weight = (remain - left) * (1.0 - 1.0 / shift)
                near = weight * lower
                far = weight * upper
                carry[4 * strip : 4 * strip + 4] = [
                    red + near * found[0] + far * found[4],
                    green + near * found[1] + far * found[5],
                    blue + near * found[2] + far * found[6],
                    left,
                ]
        return tuple(carry)

    zero = jnp.zeros((STRIP, LANES), jnp.float32)
    half_group = GROUP // 2
    wholes = lax.div(samples + (half_group - 1), GROUP)
    begin = wholes * GROUP
    done = lax.fori_loop(
        0,
        wholes,
        lambda number, carry: group(number * GROUP, GROUP, carry),
        (zero, zero, zero, zero + 1.0) * strips,
    )
    rest = (begin < samples).astype(jnp.int32)
    done = lax.fori_loop(0, rest, lambda number, carry: group(begin, half_group, carry), done)
    units = [1.0 / level for level in LEVELS[:3]] + [1.0]
    return [jnp.concatenate(done[c::4], axis=0) * units[c] for c in range(4)]


def channel_bounds(colors, density, slices):
    cover = 1.0 - jnp.exp2(
        (-1.01 * math.log2(math.e) * slices) * jnp.max(density, axis=1, keepdims=True)
    )
    most = jnp.max(colors, axis=1, keepdims=True)
    return [1.01 * cover * (most[c : c + 1] if c < 3 else 1.0) for c in range(4)]


def march_kernel(
    bins, listed, counts, vol, nxt, low, high, colors_ref, density_ref, out, vals, grads
):
    slices, rows, columns = vol.shape
    per = out.shape[3] // LANES
    colors = colors_ref[...].astype(jnp.float32)
    density = density_ref[...].astype(jnp.float32)
    pairs = packed_table(colors, density)
    out[...] = jnp.full(out.shape, -LIMIT, jnp.int16)
    scales = [2.0 * LIMIT / bound for bound in channel_bounds(colors, density, slices)]

    def per_slot(slot, carry):
        tile = listed[slot]

        @pl.when(tile >= 0)
        def _():
            prepare_tile(tile, vol, nxt, low, high, vals, grads)
            red, green, blue, remain = march_tile(
                counts[tile], pairs, vals, grads, slices, rows, bins
            )
            owner = lax.div(tile, per)
            where = pl.ds(pl.multiple_of((tile - owner * per) * LANES, LANES), LANES)
            for c, value in enumerate((red, green, blue, 1.0 - remain)):
                code = (value * scales[c] + 0.5).astype(jnp.int32) - LIMIT
                out[owner, c, :, where] = code.astype(jnp.int16)

        return carry

    lax.fori_loop(0, columns // LANES, per_slot, 0)


def halo_kernel(
    bricks, groups, vol, nxt, low, high, edges, first, last, local, send, recv
):
    b, g = lax.axis_index("view"), lax.axis_index("img")
    slices, rows, columns = vol.shape
    barrier = pltpu.get_barrier_semaphore()
    steps = [(0, 1), (0, -1), (-1, 0), (-1, 1), (-1, -1)]

    def exists(vb, vg):
        return jnp.logical_and(
            jnp.logical_and(b + vb >= 0, b + vb < bricks),
            jnp.logical_and(g + vg >= 0, g + vg < groups),
        )

    met = jnp.int32(0)
    for vb, vg in steps + [(1, 0), (1, 1), (1, -1)]:
        here = exists(vb, vg)

        @pl.when(here)
        def _(vb=vb, vg=vg):
            pl.semaphore_signal(
                barrier, inc=1, device_id=(b + vb, g + vg), device_id_type=pl.DeviceIdType.MESH
            )

        met = met + here.astype(jnp.int32)
    ends = [0, rows - PAD]
    loads = [
        pltpu.make_async_copy(vol.at[:, pl.ds(end, PAD), :], edges.at[i], local.at[i])
        for i, end in enumerate(ends)
    ]
    for load in loads:
        load.start()
    for load in loads:
        load.wait()
    for j in range(slices):
        first[j] = edges[0, j].astype(jnp.float32)[0:1]
        last[j] = edges[1, j].astype(jnp.float32)[PAD - 1 : PAD]
    pl.semaphore_wait(barrier, met)
    main, extra = pl.ds(0, slices), pl.ds(slices, 1)
    plan = [
        (last, low.at[main]),
        (first, high.at[main]),
        (vol.at[pl.ds(0, 1)], nxt),
        (last.at[pl.ds(0, 1)], low.at[extra]),
        (first.at[pl.ds(0, 1)], high.at[extra]),
    ]

    def copy(i):
        (vb, vg), (source, target) = steps[i], plan[i]
        return pltpu.make_async_remote_copy(
            src_ref=source,
            dst_ref=target,
            send_sem=send.at[i],
            recv_sem=recv.at[i],
            device_id=(b + vb, g + vg),
            device_id_type=pl.DeviceIdType.MESH,
        )

    for i, (vb, vg) in enumerate(steps):

        @pl.when(exists(vb, vg))
        def _(i=i):
            copy(i).start()

        @pl.when(jnp.logical_not(exists(-vb, -vg)))
        def _(i=i):
            plan[i][1][...] = jnp.zeros(plan[i][1].shape, plan[i][1].dtype)

    for i, (vb, vg) in enumerate(steps):

        @pl.when(exists(vb, vg))
        def _(i=i):
            copy(i).wait_send()

        @pl.when(exists(-vb, -vg))
        def _(i=i):
            copy(i).wait_recv()


def blend_kernel(bricks, slices, order, mine, colors, density, out, held, local, send, recv):
    b, g = lax.axis_index("view"), lax.axis_index("img")
    barrier = pltpu.get_barrier_semaphore()
    for step in range(1, bricks):
        pl.semaphore_signal(
            barrier,
            inc=1,
            device_id=(lax.rem(b + step, bricks), g),
            device_id_type=pl.DeviceIdType.MESH,
        )
    kept = pltpu.make_async_copy(mine.at[b], held.at[b], local)
    kept.start()
    pl.semaphore_wait(barrier, bricks - 1)
    copies = []
    for step in sorted(range(1, bricks), key=lambda r: (abs(r - bricks // 2), r)):
        peer = lax.rem(b + step, bricks)
        copies.append(
            pltpu.make_async_remote_copy(
                src_ref=mine.at[peer],
                dst_ref=held.at[b],
                send_sem=send.at[step],
                recv_sem=recv.at[step],
                device_id=(peer, g),
                device_id_type=pl.DeviceIdType.MESH,
            )
        )
        copies[-1].start()
    bounds = channel_bounds(
        colors[...].astype(jnp.float32), density[...].astype(jnp.float32), slices
    )
    rows, narrow = out.shape[1:]
    units = [jnp.broadcast_to(bound / (2.0 * LIMIT), (rows, narrow)) for bound in bounds]
    kept.wait()
    for copy in copies:
        copy.wait()

    image = [jnp.zeros((rows, narrow), jnp.float32) for _ in range(4)]
    remain = jnp.ones((rows, narrow), jnp.float32)
    for position in range(bricks):
        chosen = order[position]
        value = [
            (held[chosen, c].astype(jnp.float32) + float(LIMIT)) * units[c] for c in range(4)
        ]
        image = [image[c] + remain * value[c] for c in range(4)]
        remain = remain * (1.0 - value[3])
    for c in range(4):
        out[c] = image[c]


def shards(volume, occupied, sample_counts, depth_order, colors, density):
    slices, rows, columns = volume.shape
    bins = colors.shape[1]
    bricks, groups = lax.axis_size("view"), lax.axis_size("img")
    narrow = columns // bricks
    density = density[None, :]
    vmem = pl.BlockSpec(memory_space=pltpu.VMEM)
    smem = pl.BlockSpec(memory_space=pltpu.SMEM)
    nxt, low, high = pl.pallas_call(
        functools.partial(halo_kernel, bricks, groups),
        out_shape=(
            jax.ShapeDtypeStruct((1, rows, columns), volume.dtype),
            jax.ShapeDtypeStruct((slices + 1, 1, columns), jnp.float32),
            jax.ShapeDtypeStruct((slices + 1, 1, columns), jnp.float32),
        ),
        in_specs=[pl.BlockSpec(memory_space=pl.ANY)],
        out_specs=(vmem,) * 3,
        scratch_shapes=[
            pltpu.VMEM((2, slices, PAD, columns), volume.dtype),
            pltpu.VMEM((slices, 1, columns), jnp.float32),
            pltpu.VMEM((slices, 1, columns), jnp.float32),
            pltpu.SemaphoreType.DMA((2,)),
            pltpu.SemaphoreType.DMA((5,)),
            pltpu.SemaphoreType.DMA((5,)),
        ],
        compiler_params=pltpu.CompilerParams(
            collective_id=0, has_side_effects=True, vmem_limit_bytes=GRANT
        ),
        name="halo",
    )(volume)
    coded = pl.pallas_call(
        functools.partial(march_kernel, bins),
        out_shape=jax.ShapeDtypeStruct((bricks, 4, rows, narrow), jnp.int16),
        in_specs=[smem, smem] + [vmem] * 6,
        out_specs=vmem,
        scratch_shapes=[
            pltpu.VMEM((slices + 1, rows + 2 * PAD, LANES), jnp.float32),
            pltpu.VMEM((slices + 1, rows, LANES), jnp.float32),
        ],
        compiler_params=pltpu.CompilerParams(vmem_limit_bytes=GRANT),
        name="march",
    )(occupied[0, 0], sample_counts[0, 0], volume, nxt, low, high, colors, density)
    return pl.pallas_call(
        functools.partial(blend_kernel, bricks, slices),
        out_shape=jax.ShapeDtypeStruct((4, rows, narrow), jnp.float32),
        in_specs=[smem, vmem, vmem, vmem],
        out_specs=vmem,
        scratch_shapes=[
            pltpu.VMEM((bricks, 4, rows, narrow), jnp.int16),
            pltpu.SemaphoreType.DMA,
            pltpu.SemaphoreType.DMA((bricks,)),
            pltpu.SemaphoreType.DMA((bricks,)),
        ],
        compiler_params=pltpu.CompilerParams(
            collective_id=1, has_side_effects=True, vmem_limit_bytes=GRANT
        ),
        name="blend",
    )(depth_order, coded, colors, density)


def solution(mesh):
    return jax.shard_map(
        shards,
        mesh=mesh,
        in_specs=(
            P("view", "img", None),
            P("view", "img", None),
            P("view", "img", None),
            P(),
            P(),
            P(),
        ),
        out_specs=P(None, "img", "view"),
        check_vma=False,
    )
```

profile of v0, /device:TPU:0, one launch (start us, length us, event | category | flops | bytes accessed | tf_op | source)
XLA Modules:
  0.0 45.6 jit_solution(1915421190468902377)
XLA Ops:
  0.0 0.0 copy-start.1
  0.0 0.0 copy-start.2
  0.0 0.0 copy-start.4
  0.0 0.0 copy-start.3
  0.0 0.0 copy-start
  0.0 1.6 %copy-done = bf16[16,32,2048]{2,1,0:T(8,128)(2,1)S(1)} copy-done((bf16[16,32,2048]{2,1,0:T(8,128)(2,1)S(1)}, bf16[16,32,2048]{2,1,0:T(8,128)(2,1)}, u32[]{:S(2)}) %copy-start) | copy-done | bytes 2097176
  1.7 0.0 copy-start.5
  1.7 9.2 %halo.1 = (bf16[1,32,2048]{2,1,0:T(8,128)(2,1)S(1)}, f32[17,1,2048]{2,1,0:T(1,128)S(1)}, f32[17,1,2048]{2,1,0:T(1,128)S(1)}) custom-call(bf16[16,32,2048]{2,1,0:T(8,128)(2,1)S(1)} %copy-done), custom_call_target="tpu_custom_call" | custom-call | tf_op jit(solution)/shard_map/halo/pallas_call | solution.py:328
  10.9 0.0 copy-done.1
  10.9 0.0 copy-done.2
  10.9 0.0 copy-done.4
  10.9 0.0 copy-done.3
  10.9 19.6 %march.1.mine = s16[8,4,32,256]{3,2,1,0:T(8,128)(2,1)S(1)} custom-call(s32[16]{0:T(128)S(1)} %bitcast.5, s32[16]{0:T(128)S(1)} %bitcast.6, bf16[16,32,2048]{2,1,0:T(8,128)(2,1)S(1)} %copy-done, bf16[1,32,2048]{2,1,0:T(8,128)(2,1)S(1)} %get-tuple-element.8.nxt, f32[17,1,2048]{2,1,0:T(1,128)S(1)} %get-tuple-element.9.low, ...), custom_call_target="tpu_custom_call" | custom-call | tf_op jit(solution)/shard_map/march/pallas_call | solution.py:350
  30.5 0.0 copy-done.5
  30.5 14.4 %blend.1 = f32[4,32,256]{2,1,0:T(8,128)S(1)} custom-call(s32[8]{0:T(128)S(1)} %copy-done.5, s16[8,4,32,256]{3,2,1,0:T(8,128)(2,1)S(1)} %march.1.mine, bf16[3,128]{1,0:T(4,128)(2,1)S(1)} %copy-done.1, bf16[1,128]{1,0:T(2,128)(2,1)S(1)} %bitcast.4), custom_call_target="tpu_custom_call" | custom-call | tf_op jit(solution)/shard_map/blend/pallas_call | solution.py:362
  44.9 0.7 %copy.8 = f32[4,32,256]{2,1,0:T(8,128)} copy(f32[4,32,256]{2,1,0:T(8,128)S(1)} %blend.1) | data formatting | bytes 262144
Async XLA Ops:
  0.0 10.9 %copy-start.1 = (bf16[3,128]{1,0:T(4,128)(2,1)S(1)}, bf16[3,128]{1,0:T(4,128)(2,1)}, u32[]{:S(2)}) copy-start(bf16[3,128]{1,0:T(4,128)(2,1)} %colors.1) | copy-start | bytes 2308
  0.0 10.9 %copy-start.2 = (bf16[128]{0:T(256)(128)(2,1)S(1)}, bf16[128]{0:T(256)(128)(2,1)}, u32[]{:S(2)}) copy-start(bf16[128]{0:T(256)(128)(2,1)} %param.11) | copy-start | bytes 772
  0.0 10.9 %copy-start.4 = (s32[1,1,16]{2,1,0:T(1,128)S(1)}, s32[1,1,16]{2,1,0:T(1,128)}, u32[]{:S(2)}) copy-start(s32[1,1,16]{2,1,0:T(1,128)} %param.8) | copy-start | bytes 196
  0.0 10.9 %copy-start.3 = (s32[1,1,16]{2,1,0:T(1,128)S(1)}, s32[1,1,16]{2,1,0:T(1,128)}, u32[]{:S(2)}) copy-start(s32[1,1,16]{2,1,0:T(1,128)} %param.7) | copy-start | bytes 196
  0.0 1.6 %copy-start = (bf16[16,32,2048]{2,1,0:T(8,128)(2,1)S(1)}, bf16[16,32,2048]{2,1,0:T(8,128)(2,1)}, u32[]{:S(2)}) copy-start(bf16[16,32,2048]{2,1,0:T(8,128)(2,1)} %vol.3) | copy-start | bytes 6291460
  1.7 28.9 %copy-start.5 = (s32[8]{0:T(128)S(1)}, s32[8]{0:T(128)}, u32[]{:S(2)}) copy-start(s32[8]{0:T(128)} %order.1) | copy-start | bytes 100
where the time goes:
time: 45.8 us; the launch traced here: 45.6 us
  Pallas kernels  43.2 us (94%)
  local copies, waits for them, and re-layouts  2.32 us (5%)
    pallas_call x1, Pallas kernels, shards(): pl.pallas_call(functools.partial(march_kernel, bins), out_shape=jax.Shape...  19.6 us
    pallas_call x1, Pallas kernels, shards(): pl.pallas_call(functools.partial(blend_kernel, bricks, slices), out_shape...  14.4 us
    pallas_call x1, Pallas kernels, shards(): pl.pallas_call(functools.partial(halo_kernel, bricks, groups), out_shape=...  9.24 us
    unnamed x13, local copies, waits for them, and re-layouts  2.32 us

commit v1 on v0

v1 whole, which is shorter than its diff:
```python
import functools
import math

import jax
import jax.numpy as jnp
from jax import lax
from jax.experimental import pallas as pl
from jax.experimental.pallas import tpu as pltpu
from jax.sharding import PartitionSpec as P

LANES = 128
PAD = 8
STRIP = 8
LIMIT = 32767
MOST = 24
GROUP = 8
CHUNK = 4
GRANT = 48 * 2**20


LANE_GATHER = lax.GatherDimensionNumbers(
    offset_dims=(),
    collapsed_slice_dims=(1,),
    start_index_map=(1,),
    operand_batching_dims=(0,),
    start_indices_batching_dims=(0,),
)


def gather_lanes(row, index):
    return lax.gather(
        row, index[..., None], LANE_GATHER, (1, 1), mode=lax.GatherScatterMode.PROMISE_IN_BOUNDS
    )


def flipped(b, mask, bricks):
    result, bit = 0, 1
    while bit < bricks:
        ours, theirs = (b // bit) % 2, (mask // bit) % 2
        result = result + bit * (ours + theirs - 2 * ours * theirs)
        bit *= 2
    return result


def channel_bounds(colors, density, slices):
    cover = 1.0 - jnp.exp2(
        (-1.01 * math.log2(math.e) * slices) * jnp.max(density, axis=1, keepdims=True)
    )
    most = jnp.max(colors, axis=1, keepdims=True)
    return [1.01 * cover * (most[c : c + 1] if c < 3 else 1.0) for c in range(4)]


def lookup_tables(colors, density):
    lane = lax.broadcasted_iota(jnp.int32, (STRIP, LANES), 1)
    here = [jnp.broadcast_to(colors[c : c + 1, :], (STRIP, LANES)) for c in range(3)]
    here.append(jnp.broadcast_to(density, (STRIP, LANES)))
    after = [jnp.where(lane == LANES - 1, 0.0, pltpu.roll(t, LANES - 1, 1)) for t in here]
    return here + after


def fill_band(band):
    source = lax.broadcasted_iota(jnp.int32, band.shape, 0) - LANES
    target = lax.broadcasted_iota(jnp.int32, band.shape, 1)
    band[...] = jnp.where(
        source == target + 1, 0.5, jnp.where(source == target - 1, -0.5, 0.0)
    ).astype(band.dtype)


def along_squares(padded, at, count, tile, band):
    rows = padded.shape[1]
    blocks = [
        padded[at : at + count, :, pl.ds(pl.multiple_of((tile + i) * LANES, LANES), LANES)].reshape(
            count * rows, LANES
        )
        for i in range(3)
    ]
    along = jnp.dot(
        jnp.concatenate(blocks, axis=1), band[...], preferred_element_type=jnp.float32
    ).reshape(count, rows, LANES)
    return along * along, blocks[1].astype(jnp.float32).reshape(count, rows, LANES)


def prepare(tile, padded, first, count, at, band, vals, grads):
    rows = padded.shape[1]
    square, mid = along_squares(padded, at, count, tile, band)
    for j in range(count):
        vals[tile, first + j, PAD : PAD + rows, :] = mid[j] * 0.5
    inner = slice(STRIP, rows - STRIP)
    for j in range(count):
        z = first + j
        across = (
            vals[tile, z, PAD + STRIP + 1 : PAD + rows - STRIP + 1, :]
            - vals[tile, z, PAD + STRIP - 1 : PAD + rows - STRIP - 1, :]
        )
        grads[tile, z, 0:STRIP, :] = square[j, 0:STRIP]
        grads[tile, z, inner, :] = (across * across + square[j, inner]) * (1.0 / 0.6) + (1.0 / 0.6)
        grads[tile, z, rows - STRIP : rows, :] = square[j, rows - STRIP : rows]


def close_edges(tile, low, high, vals, grads):
    slices, rows = grads.shape[1:3]
    here = pl.ds(pl.multiple_of(tile * LANES, LANES), LANES)
    for z in range(slices):
        vals[tile, z, PAD - 1 : PAD, :] = low[z, :, here] * 0.5
        vals[tile, z, PAD + rows : PAD + rows + 1, :] = high[z, :, here] * 0.5
    for z in range(slices):
        for start in (0, rows - STRIP):
            across = (
                vals[tile, z, PAD + start + 1 : PAD + start + 1 + STRIP, :]
                - vals[tile, z, PAD + start - 1 : PAD + start - 1 + STRIP, :]
            )
            grads[tile, z, start : start + STRIP, :] = (
                across * across + grads[tile, z, start : start + STRIP, :]
            ) * (1.0 / 0.6) + (1.0 / 0.6)


def march_tile(tile, samples, shown, tables, vals, grads, bins):
    slices, rows = grads.shape[1] - 1, grads.shape[2]
    inverse = 1.0 / jnp.full((STRIP, LANES), samples.astype(jnp.float32))
    extinct = (-slices * math.log2(math.e)) * inverse
    scaled = lax.div(65535 + samples, samples)
    half = 0.5 * (bins - 1)
    strips = rows // STRIP

    def group(number, carry):
        carry = list(carry)
        for inner in range(GROUP):
            k = number * GROUP + inner
            travel = jnp.minimum(k + 1, samples) * slices
            base = jnp.minimum(lax.shift_right_logical(travel * scaled, 16), slices - 1)
            part = (travel - base * samples).astype(jnp.float32) * inverse
            rate = jnp.where(k < shown, 1.0, 0.0) * extinct
            for strip in range(strips):
                red, green, blue, remain = carry[4 * strip : 4 * strip + 4]
                v0 = vals[tile, base, pl.ds(PAD + strip * STRIP, STRIP), :]
                v1 = vals[tile, base + 1, pl.ds(PAD + strip * STRIP, STRIP), :]
                q0 = grads[tile, base, pl.ds(strip * STRIP, STRIP), :]
                q1 = grads[tile, base + 1, pl.ds(strip * STRIP, STRIP), :]
                level = half * jnp.tanh(v0 + part * (v1 - v0)) + half
                shift = q0 + part * (q1 - q0)
                index = level.astype(jnp.int32)
                frac = level - index.astype(jnp.float32)
                both = jnp.concatenate([frac, 1.0 - frac], axis=0)
                both = both.astype(jnp.bfloat16).astype(jnp.float32)
                upper, lower = both[:STRIP], both[STRIP:]
                found = [gather_lanes(table, index) for table in tables]
                sigma = lower * found[3] + upper * found[7]
                left = remain * jnp.exp2(sigma * rate)
                weight = (remain - left) * (1.0 - 1.0 / shift)
                near = weight * lower
                far = weight * upper
                carry[4 * strip : 4 * strip + 4] = [
                    red + near * found[0] + far * found[4],
                    green + near * found[1] + far * found[5],
                    blue + near * found[2] + far * found[6],
                    left,
                ]
        return tuple(carry)

    zero = jnp.zeros((STRIP, LANES), jnp.float32)
    done = lax.fori_loop(0, MOST // GROUP, group, (zero, zero, zero, zero + 1.0) * strips)
    red, green, blue, remain = [jnp.concatenate(done[c::4], axis=0) for c in range(4)]
    return red, green, blue, 1.0 - remain


def render_kernel(
    bricks,
    groups,
    listed,
    counts,
    order,
    vol,
    colors_ref,
    density_ref,
    out,
    padded,
    nxt,
    low,
    high,
    first,
    last,
    band,
    vals,
    grads,
    mine,
    held,
    load,
    send,
    recv,
    give,
    take,
):
    b, g = lax.axis_index("view"), lax.axis_index("img")
    slices, rows, columns = vol.shape
    tiles = columns // LANES
    per = tiles // bricks
    bins = colors_ref.shape[1]
    barrier = pltpu.get_barrier_semaphore()
    steps = [(-1, 0), (0, 1), (0, -1), (-1, 1), (-1, -1)]

    def exists(vb, vg):
        return jnp.logical_and(
            jnp.logical_and(b + vb >= 0, b + vb < bricks),
            jnp.logical_and(g + vg >= 0, g + vg < groups),
        )

    def greet(vb, vg):
        pl.semaphore_signal(
            barrier, inc=1, device_id=(vb, vg), device_id_type=pl.DeviceIdType.MESH
        )

    met = jnp.int32(bricks - 1)
    for step in range(1, bricks):
        greet(lax.rem(b + step, bricks), g)
    for vb, vg in [(0, 1), (0, -1), (-1, 1), (-1, -1), (1, 1), (1, -1)]:
        here = exists(vb, vg)

        @pl.when(here)
        def _(vb=vb, vg=vg):
            greet(b + vb, g + vg)

        met = met + here.astype(jnp.int32)

    middle = pl.ds(LANES, columns)
    loads = [
        pltpu.make_async_copy(
            vol.at[pl.ds(at, CHUNK)], padded.at[pl.ds(at, CHUNK), :, middle], load.at[at // CHUNK]
        )
        for at in range(0, slices, CHUNK)
    ]
    for copy in loads:
        copy.start()
    for side in (0, LANES + columns):
        padded[:, :, side : side + LANES] = jnp.zeros((slices, rows, LANES), padded.dtype)
        nxt[:, :, side : side + LANES] = jnp.zeros((1, rows, LANES), nxt.dtype)
    fill_band(band)
    colors = colors_ref[...].astype(jnp.float32)
    density = density_ref[...].astype(jnp.float32)
    tables = lookup_tables(colors, density)
    bounds = channel_bounds(colors, density, slices)
    for copy in loads:
        copy.wait()
    for j in range(slices):
        first[j] = padded[j, 0:STRIP, middle].astype(jnp.float32)[0:1]
        last[j] = padded[j, rows - STRIP : rows, middle].astype(jnp.float32)[STRIP - 1 : STRIP]
    pl.semaphore_wait(barrier, met)

    main, extra = pl.ds(0, slices), pl.ds(slices, 1)
    plan = [
        (vol.at[pl.ds(0, 1)], nxt.at[:, :, middle]),
        (last, low.at[main]),
        (first, high.at[main]),
        (last.at[pl.ds(0, 1)], low.at[extra]),
        (first.at[pl.ds(0, 1)], high.at[extra]),
    ]

    def halo(i):
        (vb, vg), (source, target) = steps[i], plan[i]
        return pltpu.make_async_remote_copy(
            src_ref=source,
            dst_ref=target,
            send_sem=send.at[i],
            recv_sem=recv.at[i],
            device_id=(b + vb, g + vg),
            device_id_type=pl.DeviceIdType.MESH,
        )

    for i, (vb, vg) in enumerate(steps):

        @pl.when(exists(vb, vg))
        def _(i=i):
            halo(i).start()

        @pl.when(jnp.logical_not(exists(-vb, -vg)))
        def _(i=i):
            plan[i][1][...] = jnp.zeros(plan[i][1].shape, plan[i][1].dtype)

    def ready(tile, carry):
        for at in range(0, slices, slices):
            prepare(tile, padded, at, slices, at, band, vals, grads)
        return carry

    lax.fori_loop(0, tiles, ready, 0)

    for i, (vb, vg) in enumerate(steps):

        @pl.when(exists(-vb, -vg))
        def _(i=i):
            halo(i).wait_recv()

    def ready_next(tile, carry):
        prepare(tile, nxt, slices, 1, 0, band, vals, grads)
        return carry

    lax.fori_loop(0, tiles, ready_next, 0)

    scales = [2.0 * LIMIT / bound for bound in bounds]

    def place(i):
        mask, part = bricks - 1 - i // per, i % per
        peer = flipped(b, mask, bricks)
        return mask, part, peer

    def give_away(i):
        mask, part, peer = place(i)
        return pltpu.make_async_remote_copy(
            src_ref=mine.at[peer * per + part],
            dst_ref=held.at[b, part],
            send_sem=give.at[mask, part],
            recv_sem=take.at[mask, part],
            device_id=(peer, g),
            device_id_type=pl.DeviceIdType.MESH,
        )

    def march(i, carry):
        _, part, peer = place(i)
        tile = peer * per + part
        samples = counts[tile]
        live = jnp.int32(0)
        for slot in range(tiles):
            live = jnp.maximum(live, (listed[slot] == tile).astype(jnp.int32))
        close_edges(tile, low, high, vals, grads)
        result = march_tile(tile, samples, live * samples, tables, vals, grads, bins)
        for c, value in enumerate(result):
            code = (value * scales[c] + 0.5).astype(jnp.int32) - LIMIT
            mine[tile, c] = code.astype(jnp.int16)

        @pl.when(jnp.logical_and(i >= 1, i <= (bricks - 1) * per))
        def _():
            give_away(i - 1).start()

        return carry

    lax.fori_loop(0, tiles, march, 0)
    for part in range(per):
        held[b, part] = mine[b * per + part]
    units = [jnp.broadcast_to(bound / (2.0 * LIMIT), (rows, LANES)) for bound in bounds]
    for i, (vb, vg) in enumerate(steps):

        @pl.when(exists(vb, vg))
        def _(i=i):
            halo(i).wait_send()

    for i in range((bricks - 1) * per):
        give_away(i).wait()

    for part in range(per):
        image = [jnp.zeros((rows, LANES), jnp.float32) for _ in range(4)]
        remain = jnp.ones((rows, LANES), jnp.float32)
        for position in range(bricks):
            chosen = order[position]
            value = [
                (held[chosen, part, c].astype(jnp.float32) + float(LIMIT)) * units[c]
                for c in range(4)
            ]
            image = [image[c] + remain * value[c] for c in range(4)]
            remain = remain * (1.0 - value[3])
        for c in range(4):
            out[c, :, part * LANES : (part + 1) * LANES] = image[c]


def shards(volume, occupied, sample_counts, depth_order, colors, density):
    slices, rows, columns = volume.shape
    bricks, groups = lax.axis_size("view"), lax.axis_size("img")
    tiles = columns // LANES
    per = tiles // bricks
    vmem = pl.BlockSpec(memory_space=pltpu.VMEM)
    smem = pl.BlockSpec(memory_space=pltpu.SMEM)
    hbm = pl.BlockSpec(memory_space=pltpu.HBM)
    return pl.pallas_call(
        functools.partial(render_kernel, bricks, groups),
        out_shape=jax.ShapeDtypeStruct((4, rows, per * LANES), jnp.float32),
        in_specs=[smem, smem, smem, hbm, vmem, vmem],
        out_specs=vmem,
        scratch_shapes=[
            pltpu.VMEM((slices, rows, columns + 2 * LANES), volume.dtype),
            pltpu.VMEM((1, rows, columns + 2 * LANES), volume.dtype),
            pltpu.VMEM((slices + 1, 1, columns), jnp.float32),
            pltpu.VMEM((slices + 1, 1, columns), jnp.float32),
            pltpu.VMEM((slices, 1, columns), jnp.float32),
            pltpu.VMEM((slices, 1, columns), jnp.float32),
            pltpu.VMEM((3 * LANES, LANES), jnp.bfloat16),
            pltpu.VMEM((tiles, slices + 1, rows + 2 * PAD, LANES), jnp.float32),
            pltpu.VMEM((tiles, slices + 1, rows, LANES), jnp.float32),
            pltpu.VMEM((tiles, 4, rows, LANES), jnp.int16),
            pltpu.VMEM((bricks, per, 4, rows, LANES), jnp.int16),
            pltpu.SemaphoreType.DMA((slices // CHUNK,)),
            pltpu.SemaphoreType.DMA((5,)),
            pltpu.SemaphoreType.DMA((5,)),
            pltpu.SemaphoreType.DMA((bricks, per)),
            pltpu.SemaphoreType.DMA((bricks, per)),
        ],
        compiler_params=pltpu.CompilerParams(
            collective_id=0, has_side_effects=True, vmem_limit_bytes=GRANT
        ),
        name="render",
    )(occupied[0, 0], sample_counts[0, 0], depth_order, volume, colors, density[None, :])


def solution(mesh):
    return jax.shard_map(
        shards,
        mesh=mesh,
        in_specs=(
            P("view", "img", None),
            P("view", "img", None),
            P("view", "img", None),
            P(),
            P(),
            P(),
        ),
        out_specs=P(None, "img", "view"),
        check_vma=False,
    )
```

time: 45.8 us -> 46.3 us (1.011)
  local copies, waits for them, and re-layouts: 2.32 us -> 5.55 us
  Pallas kernels: 43.2 us -> 40.5 us
    unnamed x13, local copies, waits for them, and re-layouts: 2.32 us -> 5.55 us
    pallas_call x3 -> x1, Pallas kernels: 43.2 us -> 40.5 us  [shards(): pl.pallas_call(functools.partial(render_kernel, bricks, groups), out_shap...]
where the time goes in v1:
time: 46.3 us; the launch traced here: 46.1 us
  Pallas kernels  40.5 us (87%)
  local copies, waits for them, and re-layouts  5.55 us (12%)
    pallas_call x1, Pallas kernels, shards(): pl.pallas_call(functools.partial(render_kernel, bricks, groups), out_shap...  40.5 us
    unnamed x13, local copies, waits for them, and re-layouts  5.55 us

profile of v1, /device:TPU:0, one launch (start us, length us, event | category | flops | bytes accessed | tf_op | source)
XLA Modules:
  0.0 46.1 jit_solution(17139205584951638632)
XLA Ops:
  0.0 0.0 copy-start
  0.0 1.6 %copy-done = bf16[16,32,2048]{2,1,0:T(8,128)(2,1)S(1)} copy-done((bf16[16,32,2048]{2,1,0:T(8,128)(2,1)S(1)}, bf16[16,32,2048]{2,1,0:T(8,128)(2,1)}, u32[]{:S(2)}) %copy-start) | copy-done | bytes 2097176
  1.6 0.0 copy-start.1
  1.6 0.7 %copy-done.1 = bf16[3,128]{1,0:T(4,128)(2,1)S(1)} copy-done((bf16[3,128]{1,0:T(4,128)(2,1)S(1)}, bf16[3,128]{1,0:T(4,128)(2,1)}, u32[]{:S(2)}) %copy-start.1) | copy-done | bytes 792
  2.3 0.0 copy-start.2
  2.3 0.7 %copy-done.2 = s32[1,1,16]{2,1,0:T(1,128)S(1)} copy-done((s32[1,1,16]{2,1,0:T(1,128)S(1)}, s32[1,1,16]{2,1,0:T(1,128)}, u32[]{:S(2)}) %copy-start.2) | copy-done | bytes 88
  2.9 0.0 copy-start.3
  2.9 0.7 %copy-done.3 = s32[1,1,16]{2,1,0:T(1,128)S(1)} copy-done((s32[1,1,16]{2,1,0:T(1,128)S(1)}, s32[1,1,16]{2,1,0:T(1,128)}, u32[]{:S(2)}) %copy-start.3) | copy-done | bytes 88
  3.6 0.0 copy-start.4
  3.6 0.7 %copy-done.4 = s32[8]{0:T(128)S(1)} copy-done((s32[8]{0:T(128)S(1)}, s32[8]{0:T(128)}, u32[]{:S(2)}) %copy-start.4) | copy-done | bytes 56
  4.2 0.0 copy-start.5
  4.2 0.7 %copy-done.5 = bf16[128]{0:T(256)(128)(2,1)S(1)} copy-done((bf16[128]{0:T(256)(128)(2,1)S(1)}, bf16[128]{0:T(256)(128)(2,1)}, u32[]{:S(2)}) %copy-start.5) | copy-done | bytes 280
  4.9 40.5 %render.1 = f32[4,32,256]{2,1,0:T(8,128)S(1)} custom-call(s32[16]{0:T(128)S(1)} %bitcast.3, s32[16]{0:T(128)S(1)} %bitcast.4, s32[8]{0:T(128)S(1)} %copy-done.4, bf16[16,32,2048]{2,1,0:T(8,128)(2,1)S(1)} %copy-done, bf16[3,128]{1,0:T(4,128)(2,1)S(1)} %copy-done.1, bf16[1,128]{1,0:T(2,128)(2,1)S(1)} %bitcast.5), custom_call_target="tpu_custom_call" | custom-call | tf_op jit(solution)/shard_map/render/pallas_call | solution.py:370
  45.4 0.7 %copy.8 = f32[4,32,256]{2,1,0:T(8,128)} copy(f32[4,32,256]{2,1,0:T(8,128)S(1)} %render.1) | data formatting | bytes 262144
Async XLA Ops:
  0.0 1.6 %copy-start = (bf16[16,32,2048]{2,1,0:T(8,128)(2,1)S(1)}, bf16[16,32,2048]{2,1,0:T(8,128)(2,1)}, u32[]{:S(2)}) copy-start(bf16[16,32,2048]{2,1,0:T(8,128)(2,1)} %vol.1) | copy-start | bytes 6291460
  1.6 0.7 %copy-start.1 = (bf16[3,128]{1,0:T(4,128)(2,1)S(1)}, bf16[3,128]{1,0:T(4,128)(2,1)}, u32[]{:S(2)}) copy-start(bf16[3,128]{1,0:T(4,128)(2,1)} %colors_ref.1) | copy-start | bytes 2308
  2.3 0.7 %copy-start.2 = (s32[1,1,16]{2,1,0:T(1,128)S(1)}, s32[1,1,16]{2,1,0:T(1,128)}, u32[]{:S(2)}) copy-start(s32[1,1,16]{2,1,0:T(1,128)} %param.7) | copy-start | bytes 196
  2.9 0.7 %copy-start.3 = (s32[1,1,16]{2,1,0:T(1,128)S(1)}, s32[1,1,16]{2,1,0:T(1,128)}, u32[]{:S(2)}) copy-start(s32[1,1,16]{2,1,0:T(1,128)} %param.8) | copy-start | bytes 196
  3.6 0.7 %copy-start.4 = (s32[8]{0:T(128)S(1)}, s32[8]{0:T(128)}, u32[]{:S(2)}) copy-start(s32[8]{0:T(128)} %order.1) | copy-start | bytes 100
  4.2 0.7 %copy-start.5 = (bf16[128]{0:T(256)(128)(2,1)S(1)}, bf16[128]{0:T(256)(128)(2,1)}, u32[]{:S(2)}) copy-start(bf16[128]{0:T(256)(128)(2,1)} %param.11) | copy-start | bytes 772

commit v2 on v1

--- a/solution.py
+++ b/solution.py
@@ -14,8 +14,11 @@
 LIMIT = 32767
 MOST = 24
 GROUP = 8
+ROUNDS = MOST // GROUP
+LEVEL = 4096.0
+FINE = 65536.0
 CHUNK = 4
-GRANT = 48 * 2**20
+GRANT = 67043328
 
 
 LANE_GATHER = lax.GatherDimensionNumbers(
@@ -51,11 +54,31 @@
 
 
 def lookup_tables(colors, density):
-    lane = lax.broadcasted_iota(jnp.int32, (STRIP, LANES), 1)
-    here = [jnp.broadcast_to(colors[c : c + 1, :], (STRIP, LANES)) for c in range(3)]
-    here.append(jnp.broadcast_to(density, (STRIP, LANES)))
-    after = [jnp.where(lane == LANES - 1, 0.0, pltpu.roll(t, LANES - 1, 1)) for t in here]
-    return here + after
+    entries = [colors[c : c + 1, :] * LEVEL - 1.0 for c in range(3)] + [density * FINE]
+    pairs = []
+    for entry in entries:
+        here = jnp.broadcast_to(entry, (STRIP, LANES))
+        pairs.append(here + pltpu.roll(here, LANES - 1, 1) * (1.0 / LEVEL))
+    return pairs
+
+
+def sample_plan(listed, counts, slices, tiles):
+    shape = (MOST, LANES)
+    lane = lax.broadcasted_iota(jnp.int32, shape, 1)
+    count = jnp.ones(shape, jnp.int32)
+    shown = jnp.zeros(shape, jnp.int32)
+    for tile in range(tiles):
+        count = jnp.where(lane == tile, jnp.maximum(counts[0, 0, tile], 1), count)
+    for slot in range(tiles):
+        shown = jnp.where(lane == listed[0, 0, slot], count, shown)
+    k = lax.broadcasted_iota(jnp.int32, shape, 0)
+    travel = jnp.minimum(k + 1, count) * slices
+    whole = count.astype(jnp.float32)
+    base = ((travel.astype(jnp.float32) + 0.5) / whole).astype(jnp.int32)
+    base = jnp.clip(base, 0, slices - 1)
+    part = (travel - base * count).astype(jnp.float32) / whole
+    rate = jnp.where(k < shown, (-slices * math.log2(math.e) / FINE) / whole, 0.0)
+    return jnp.minimum(lane, tiles - 1) * (slices + 1) + base, part, rate
 
 
 def fill_band(band):
@@ -80,99 +103,101 @@
     return along * along, blocks[1].astype(jnp.float32).reshape(count, rows, LANES)
 
 
-def prepare(tile, padded, first, count, at, band, vals, grads):
+def prepare(tile, depth, padded, first, count, at, band, vals, grads):
     rows = padded.shape[1]
     square, mid = along_squares(padded, at, count, tile, band)
     for j in range(count):
-        vals[tile, first + j, PAD : PAD + rows, :] = mid[j] * 0.5
+        vals[tile * depth + first + j, PAD : PAD + rows, :] = mid[j] * 0.5
     inner = slice(STRIP, rows - STRIP)
     for j in range(count):
         z = first + j
         across = (
-            vals[tile, z, PAD + STRIP + 1 : PAD + rows - STRIP + 1, :]
-            - vals[tile, z, PAD + STRIP - 1 : PAD + rows - STRIP - 1, :]
-        )
-        grads[tile, z, 0:STRIP, :] = square[j, 0:STRIP]
-        grads[tile, z, inner, :] = (across * across + square[j, inner]) * (1.0 / 0.6) + (1.0 / 0.6)
-        grads[tile, z, rows - STRIP : rows, :] = square[j, rows - STRIP : rows]
+            vals[tile * depth + z, PAD + STRIP + 1 : PAD + rows - STRIP + 1, :]
+            - vals[tile * depth + z, PAD + STRIP - 1 : PAD + rows - STRIP - 1, :]
+        )
+        grads[tile * depth + z, 0:STRIP, :] = square[j, 0:STRIP]
+        grads[tile * depth + z, inner, :] = (across * across + square[j, inner]) * (1.0 / 0.6) + (1.0 / 0.6)
+        grads[tile * depth + z, rows - STRIP : rows, :] = square[j, rows - STRIP : rows]
 
 
 def close_edges(tile, low, high, vals, grads):
-    slices, rows = grads.shape[1:3]
+    depth, rows = low.shape[0], grads.shape[1]
     here = pl.ds(pl.multiple_of(tile * LANES, LANES), LANES)
-    for z in range(slices):
-        vals[tile, z, PAD - 1 : PAD, :] = low[z, :, here] * 0.5
-        vals[tile, z, PAD + rows : PAD + rows + 1, :] = high[z, :, here] * 0.5
-    for z in range(slices):
+    for z in range(depth):
+        vals[tile * depth + z, PAD - 1 : PAD, :] = low[z, :, here] * 0.5
+        vals[tile * depth + z, PAD + rows : PAD + rows + 1, :] = high[z, :, here] * 0.5
+    for z in range(depth):
         for start in (0, rows - STRIP):
             across = (
-                vals[tile, z, PAD + start + 1 : PAD + start + 1 + STRIP, :]
-                - vals[tile, z, PAD + start - 1 : PAD + start - 1 + STRIP, :]
+                vals[tile * depth + z, PAD + start + 1 : PAD + start + 1 + STRIP, :]
+                - vals[tile * depth + z, PAD + start - 1 : PAD + start - 1 + STRIP, :]
             )
-            grads[tile, z, start : start + STRIP, :] = (
-                across * across + grads[tile, z, start : start + STRIP, :]
+            grads[tile * depth + z, start : start + STRIP, :] = (
+                across * across + grads[tile * depth + z, start : start + STRIP, :]
             ) * (1.0 / 0.6) + (1.0 / 0.6)
 
 
-def march_tile(tile, samples, shown, tables, vals, grads, bins):
-    slices, rows = grads.shape[1] - 1, grads.shape[2]
-    inverse = 1.0 / jnp.full((STRIP, LANES), samples.astype(jnp.float32))
-    extinct = (-slices * math.log2(math.e)) * inverse
-    scaled = lax.div(65535 + samples, samples)
-    half = 0.5 * (bins - 1)
-    strips = rows // STRIP
-
-    def group(number, carry):
-        carry = list(carry)
-        for inner in range(GROUP):
-            k = number * GROUP + inner
-            travel = jnp.minimum(k + 1, samples) * slices
-            base = jnp.minimum(lax.shift_right_logical(travel * scaled, 16), slices - 1)
-            part = (travel - base * samples).astype(jnp.float32) * inverse
-            rate = jnp.where(k < shown, 1.0, 0.0) * extinct
-            for strip in range(strips):
-                red, green, blue, remain = carry[4 * strip : 4 * strip + 4]
-                v0 = vals[tile, base, pl.ds(PAD + strip * STRIP, STRIP), :]
-                v1 = vals[tile, base + 1, pl.ds(PAD + strip * STRIP, STRIP), :]
-                q0 = grads[tile, base, pl.ds(strip * STRIP, STRIP), :]
-                q1 = grads[tile, base + 1, pl.ds(strip * STRIP, STRIP), :]
-                level = half * jnp.tanh(v0 + part * (v1 - v0)) + half
-                shift = q0 + part * (q1 - q0)
-                index = level.astype(jnp.int32)
-                frac = level - index.astype(jnp.float32)
-                both = jnp.concatenate([frac, 1.0 - frac], axis=0)
-                both = both.astype(jnp.bfloat16).astype(jnp.float32)
-                upper, lower = both[:STRIP], both[STRIP:]
-                found = [gather_lanes(table, index) for table in tables]
-                sigma = lower * found[3] + upper * found[7]
-                left = remain * jnp.exp2(sigma * rate)
-                weight = (remain - left) * (1.0 - 1.0 / shift)
-                near = weight * lower
-                far = weight * upper
-                carry[4 * strip : 4 * strip + 4] = [
-                    red + near * found[0] + far * found[4],
-                    green + near * found[1] + far * found[5],
-                    blue + near * found[2] + far * found[6],
-                    left,
-                ]
-        return tuple(carry)
-
-    zero = jnp.zeros((STRIP, LANES), jnp.float32)
-    done = lax.fori_loop(0, MOST // GROUP, group, (zero, zero, zero, zero + 1.0) * strips)
-    red, green, blue, remain = [jnp.concatenate(done[c::4], axis=0) for c in range(4)]
-    return red, green, blue, 1.0 - remain
+def levels(tile, number, places, parts, vals, grads, half, cells, weights, shades):
+    strips = grads.shape[1] // STRIP
+    for inner in range(GROUP):
+        here = pl.ds(places[number * GROUP + inner, tile], 2)
+        part = parts[number * GROUP + inner, tile]
+        for strip in range(strips):
+            unit = inner * strips + strip
+            v = vals[here, PAD + strip * STRIP : PAD + (strip + 1) * STRIP, :]
+            q = grads[here, strip * STRIP : (strip + 1) * STRIP, :]
+            level = half * jnp.tanh(v[0] + part * (v[1] - v[0])) + half
+            shift = q[0] + part * (q[1] - q[0])
+            index = level.astype(jnp.int32)
+            frac = level - index.astype(jnp.float32)
+            cells[number, unit] = index
+            weights[number, unit] = jnp.concatenate([frac, 1.0 - frac], axis=0).astype(jnp.bfloat16)
+            shades[number, unit] = 1.0 - 1.0 / shift
+
+
+def composite(tile, number, rates, pairs, cells, weights, shades, carry):
+    strips = len(carry)
+    for inner in range(GROUP):
+        rate = rates[number * GROUP + inner, tile]
+        for strip in range(strips):
+            unit = inner * strips + strip
+            remain, nears, fars, paint = carry[strip]
+            index = cells[number, unit]
+            both = weights[number, unit].astype(jnp.float32)
+            upper, lower = both[:STRIP] * LEVEL, both[STRIP:]
+            found = [gather_lanes(pair, index) for pair in pairs]
+            whole = [jnp.floor(value) for value in found]
+            after = [value - first for value, first in zip(found, whole)]
+            sigma = lower * whole[3] + upper * after[3]
+            left = remain * jnp.exp2(sigma * rate)
+            weight = (remain - left) * shades[number, unit]
+            near = weight * lower
+            far = weight * upper
+            paint = [paint[c] + near * whole[c] + far * after[c] for c in range(3)]
+            carry[strip] = (left, nears + near, fars + far, paint)
+    return carry
 
 
 def render_kernel(
     bricks,
     groups,
+    listed_in,
+    counts_in,
+    order_in,
+    vol,
+    colors_in,
+    density_in,
+    out,
     listed,
     counts,
     order,
-    vol,
+    places,
+    parts,
+    rates,
     colors_ref,
     density_ref,
-    out,
+    rows_of,
+    reals,
     padded,
     nxt,
     low,
@@ -182,8 +207,12 @@
     band,
     vals,
     grads,
+    cells,
+    weights,
+    shades,
     mine,
     held,
+    small,
     load,
     send,
     recv,
@@ -194,7 +223,7 @@
     slices, rows, columns = vol.shape
     tiles = columns // LANES
     per = tiles // bricks
-    bins = colors_ref.shape[1]
+    bins = colors_in.shape[1]
     barrier = pltpu.get_barrier_semaphore()
     steps = [(-1, 0), (0, 1), (0, -1), (-1, 1), (-1, -1)]
 
@@ -228,21 +257,46 @@
         )
         for at in range(0, slices, CHUNK)
     ]
-    for copy in loads:
+    fetches = [
+        pltpu.make_async_copy(source, target, small.at[i])
+        for i, (source, target) in enumerate(
+            [
+                (colors_in, colors_ref),
+                (density_in, density_ref),
+                (counts_in, counts),
+                (listed_in, listed),
+                (order_in, order),
+            ]
+        )
+    ]
+    for copy in loads + fetches:
         copy.start()
     for side in (0, LANES + columns):
         padded[:, :, side : side + LANES] = jnp.zeros((slices, rows, LANES), padded.dtype)
         nxt[:, :, side : side + LANES] = jnp.zeros((1, rows, LANES), nxt.dtype)
     fill_band(band)
+    for copy in fetches:
+        copy.wait()
     colors = colors_ref[...].astype(jnp.float32)
     density = density_ref[...].astype(jnp.float32)
-    tables = lookup_tables(colors, density)
+    pairs = lookup_tables(colors, density)
+    plans = sample_plan(listed, counts, slices, tiles)
+    for i, plan_of in enumerate(plans):
+        (rows_of if i == 0 else reals.at[i - 1])[...] = plan_of
     bounds = channel_bounds(colors, density, slices)
     for copy in loads:
         copy.wait()
     for j in range(slices):
         first[j] = padded[j, 0:STRIP, middle].astype(jnp.float32)[0:1]
         last[j] = padded[j, rows - STRIP : rows, middle].astype(jnp.float32)[STRIP - 1 : STRIP]
+    tables = [
+        pltpu.make_async_copy(source, target, small.at[5 + i])
+        for i, (source, target) in enumerate(
+            [(rows_of, places), (reals.at[0], parts), (reals.at[1], rates)]
+        )
+    ]
+    for copy in tables:
+        copy.start()
     pl.semaphore_wait(barrier, met)
 
     main, extra = pl.ds(0, slices), pl.ds(slices, 1)
@@ -277,7 +331,7 @@
 
     def ready(tile, carry):
         for at in range(0, slices, slices):
-            prepare(tile, padded, at, slices, at, band, vals, grads)
+            prepare(tile, slices + 1, padded, at, slices, at, band, vals, grads)
         return carry
 
     lax.fori_loop(0, tiles, ready, 0)
@@ -288,8 +342,11 @@
         def _(i=i):
             halo(i).wait_recv()
 
+    for copy in tables:
+        copy.wait()
+
     def ready_next(tile, carry):
-        prepare(tile, nxt, slices, 1, 0, band, vals, grads)
+        prepare(tile, slices + 1, nxt, slices, 1, 0, band, vals, grads)
         return carry
 
     lax.fori_loop(0, tiles, ready_next, 0)
@@ -312,15 +369,34 @@
             device_id_type=pl.DeviceIdType.MESH,
         )
 
+    def tile_of(i):
+        _, part, peer = place(i)
+        return peer * per + part
+
+    half = 0.5 * (bins - 1)
+
+    def closed(tile, carry):
+        close_edges(tile, low, high, vals, grads)
+        return carry
+
+    lax.fori_loop(0, tiles, closed, 0)
+    levels(tile_of(0), 0, places, parts, vals, grads, half, cells, weights, shades)
+
     def march(i, carry):
-        _, part, peer = place(i)
-        tile = peer * per + part
-        samples = counts[tile]
-        live = jnp.int32(0)
-        for slot in range(tiles):
-            live = jnp.maximum(live, (listed[slot] == tile).astype(jnp.int32))
-        close_edges(tile, low, high, vals, grads)
-        result = march_tile(tile, samples, live * samples, tables, vals, grads, bins)
+        tile = tile_of(i)
+        zero = jnp.zeros((STRIP, LANES), jnp.float32)
+        state = [(zero + 1.0, zero, zero, [zero] * 3) for _ in range(rows // STRIP)]
+        for number in range(ROUNDS):
+            if number + 1 < ROUNDS:
+                levels(tile, number + 1, places, parts, vals, grads, half, cells, weights, shades)
+            state = composite(tile, number, rates, pairs, cells, weights, shades, state)
+        after = tile_of(jnp.minimum(i + 1, tiles - 1))
+        levels(after, 0, places, parts, vals, grads, half, cells, weights, shades)
+        result = []
+        for c in range(3):
+            paint = [paint[c] + nears + fars * (1.0 / LEVEL) for _, nears, fars, paint in state]
+            result.append(jnp.concatenate(paint, axis=0) * (1.0 / LEVEL))
+        result.append(1.0 - jnp.concatenate([remain for remain, *_ in state], axis=0))
         for c, value in enumerate(result):
             code = (value * scales[c] + 0.5).astype(jnp.int32) - LIMIT
             mine[tile, c] = code.astype(jnp.int16)
@@ -365,14 +441,23 @@
     tiles = columns // LANES
     per = tiles // bricks
     vmem = pl.BlockSpec(memory_space=pltpu.VMEM)
-    smem = pl.BlockSpec(memory_space=pltpu.SMEM)
     hbm = pl.BlockSpec(memory_space=pltpu.HBM)
     return pl.pallas_call(
         functools.partial(render_kernel, bricks, groups),
         out_shape=jax.ShapeDtypeStruct((4, rows, per * LANES), jnp.float32),
-        in_specs=[smem, smem, smem, hbm, vmem, vmem],
+        in_specs=[hbm] * 6,
         out_specs=vmem,
         scratch_shapes=[
+            pltpu.SMEM(occupied.shape, jnp.int32),
+            pltpu.SMEM(sample_counts.shape, jnp.int32),
+            pltpu.SMEM(depth_order.shape, jnp.int32),
+            pltpu.SMEM((MOST, LANES), jnp.int32),
+            pltpu.SMEM((MOST, LANES), jnp.float32),
+            pltpu.SMEM((MOST, LANES), jnp.float32),
+            pltpu.VMEM(colors.shape, colors.dtype),
+            pltpu.VMEM((1, density.shape[0]), density.dtype),
+            pltpu.VMEM((MOST, LANES), jnp.int32),
+            pltpu.VMEM((2, MOST, LANES), jnp.float32),
             pltpu.VMEM((slices, rows, columns + 2 * LANES), volume.dtype),
             pltpu.VMEM((1, rows, columns + 2 * LANES), volume.dtype),
             pltpu.VMEM((slices + 1, 1, columns), jnp.float32),
@@ -380,10 +465,14 @@
             pltpu.VMEM((slices, 1, columns), jnp.float32),
             pltpu.VMEM((slices, 1, columns), jnp.float32),
             pltpu.VMEM((3 * LANES, LANES), jnp.bfloat16),
-            pltpu.VMEM((tiles, slices + 1, rows + 2 * PAD, LANES), jnp.float32),
-            pltpu.VMEM((tiles, slices + 1, rows, LANES), jnp.float32),
+            pltpu.VMEM((tiles * (slices + 1), rows + 2 * PAD, LANES), jnp.float32),
+            pltpu.VMEM((tiles * (slices + 1), rows, LANES), jnp.float32),
+            pltpu.VMEM((ROUNDS, GROUP * (rows // STRIP), STRIP, LANES), jnp.int32),
+            pltpu.VMEM((ROUNDS, GROUP * (rows // STRIP), 2 * STRIP, LANES), jnp.bfloat16),
+            pltpu.VMEM((ROUNDS, GROUP * (rows // STRIP), STRIP, LANES), jnp.float32),
             pltpu.VMEM((tiles, 4, rows, LANES), jnp.int16),
             pltpu.VMEM((bricks, per, 4, rows, LANES), jnp.int16),
+            pltpu.SemaphoreType.DMA((8,)),
             pltpu.SemaphoreType.DMA((slices // CHUNK,)),
             pltpu.SemaphoreType.DMA((5,)),
             pltpu.SemaphoreType.DMA((5,)),
@@ -394,7 +483,7 @@
             collective_id=0, has_side_effects=True, vmem_limit_bytes=GRANT
         ),
         name="render",
-    )(occupied[0, 0], sample_counts[0, 0], depth_order, volume, colors, density[None, :])
+    )(occupied, sample_counts, depth_order, volume, colors, density[None, :])
 
 
 def solution(mesh):

time: 46.3 us -> 33.2 us (0.72)
  Pallas kernels: 40.5 us -> 31.5 us
  local copies, waits for them, and re-layouts: 5.55 us -> 1.57 us
    pallas_call x1, Pallas kernels: 40.5 us -> 31.5 us  [shards(): pl.pallas_call(functools.partial(render_kernel, bricks, groups), out_shap...]
    unnamed x13 -> x1, local copies, waits for them, and re-layouts: 5.55 us -> 1.57 us
where the time goes in v2:
time: 33.2 us; the launch traced here: 33.1 us
  Pallas kernels  31.5 us (95%)
  local copies, waits for them, and re-layouts  1.57 us (5%)
    pallas_call x1, Pallas kernels, shards(): pl.pallas_call(functools.partial(render_kernel, bricks, groups), out_shap...  31.5 us
    unnamed x1, local copies, waits for them, and re-layouts  1.57 us

profile of v2, /device:TPU:0, one launch (start us, length us, event | category | flops | bytes accessed | tf_op | source)
XLA Modules:
  0.0 33.1 jit_solution(6695684520700910432)
XLA Ops:
  0.0 31.5 %render.1 = f32[4,32,256]{2,1,0:T(8,128)} custom-call(s32[1,1,16]{2,1,0:T(1,128)} %listed_in.1, s32[1,1,16]{2,1,0:T(1,128)} %counts_in.1, s32[8]{0:T(128)} %order_in.1, bf16[16,32,2048]{2,1,0:T(8,128)(2,1)} %vol.1, bf16[3,128]{1,0:T(4,128)(2,1)} %colors_in.1, bf16[1,128]{1,0:T(2,128)(2,1)} %bitcast.1), custom_call_target="tpu_custom_call" | custom-call | tf_op jit(solution)/shard_map/render/pallas_call | solution.py:445
  31.5 1.6 %copy.8 = f32[4,32,256]{2,1,0:T(8,128)} copy(f32[4,32,256]{2,1,0:T(8,128)} %render.1) | data formatting | bytes 262144

commit v3 on v2

--- a/solution.py
+++ b/solution.py
@@ -18,6 +18,8 @@
 LEVEL = 4096.0
 FINE = 65536.0
 CHUNK = 4
+QUARTERS = 4
+AHEAD = 2
 GRANT = 67043328
 
 
@@ -43,6 +45,14 @@
         result = result + bit * (ours + theirs - 2 * ours * theirs)
         bit *= 2
     return result
+
+
+def spread_circles(bricks):
+    known, circles = 1, []
+    while known < bricks - 1:
+        circles.append(known)
+        known += known
+    return circles
 
 
 def channel_bounds(colors, density, slices):
@@ -92,9 +102,9 @@
 def along_squares(padded, at, count, tile, band):
     rows = padded.shape[1]
     blocks = [
-        padded[at : at + count, :, pl.ds(pl.multiple_of((tile + i) * LANES, LANES), LANES)].reshape(
-            count * rows, LANES
-        )
+        padded[
+            pl.ds(at, count), :, pl.ds(pl.multiple_of((tile + i) * LANES, LANES), LANES)
+        ].reshape(count * rows, LANES)
         for i in range(3)
     ]
     along = jnp.dot(
@@ -103,9 +113,9 @@
     return along * along, blocks[1].astype(jnp.float32).reshape(count, rows, LANES)
 
 
-def prepare(tile, depth, padded, first, count, at, band, vals, grads):
+def prepare(tile, depth, padded, first, count, at, shift, band, vals, grads, squares):
     rows = padded.shape[1]
-    square, mid = along_squares(padded, at, count, tile, band)
+    square, mid = along_squares(padded, at, count, tile - shift, band)
     for j in range(count):
         vals[tile * depth + first + j, PAD : PAD + rows, :] = mid[j] * 0.5
     inner = slice(STRIP, rows - STRIP)
@@ -115,25 +125,25 @@
             vals[tile * depth + z, PAD + STRIP + 1 : PAD + rows - STRIP + 1, :]
             - vals[tile * depth + z, PAD + STRIP - 1 : PAD + rows - STRIP - 1, :]
         )
-        grads[tile * depth + z, 0:STRIP, :] = square[j, 0:STRIP]
+        squares[tile * depth + z, 0:STRIP, :] = square[j, 0:STRIP]
         grads[tile * depth + z, inner, :] = (across * across + square[j, inner]) * (1.0 / 0.6) + (1.0 / 0.6)
-        grads[tile * depth + z, rows - STRIP : rows, :] = square[j, rows - STRIP : rows]
-
-
-def close_edges(tile, low, high, vals, grads):
+        squares[tile * depth + z, STRIP : 2 * STRIP, :] = square[j, rows - STRIP : rows]
+
+
+def close_edges(tile, low, high, vals, grads, squares):
     depth, rows = low.shape[0], grads.shape[1]
     here = pl.ds(pl.multiple_of(tile * LANES, LANES), LANES)
     for z in range(depth):
         vals[tile * depth + z, PAD - 1 : PAD, :] = low[z, :, here] * 0.5
         vals[tile * depth + z, PAD + rows : PAD + rows + 1, :] = high[z, :, here] * 0.5
     for z in range(depth):
-        for start in (0, rows - STRIP):
+        for side, start in ((0, 0), (STRIP, rows - STRIP)):
             across = (
                 vals[tile * depth + z, PAD + start + 1 : PAD + start + 1 + STRIP, :]
                 - vals[tile * depth + z, PAD + start - 1 : PAD + start - 1 + STRIP, :]
             )
             grads[tile * depth + z, start : start + STRIP, :] = (
-                across * across + grads[tile * depth + z, start : start + STRIP, :]
+                across * across + squares[tile * depth + z, side : side + STRIP, :]
             ) * (1.0 / 0.6) + (1.0 / 0.6)
 
 
@@ -207,6 +217,7 @@
     band,
     vals,
     grads,
+    squares,
     cells,
     weights,
     shades,
@@ -218,6 +229,7 @@
     recv,
     give,
     take,
+    wider,
 ):
     b, g = lax.axis_index("view"), lax.axis_index("img")
     slices, rows, columns = vol.shape
@@ -225,6 +237,7 @@
     per = tiles // bricks
     bins = colors_in.shape[1]
     barrier = pltpu.get_barrier_semaphore()
+    circles = spread_circles(bricks)
     steps = [(-1, 0), (0, 1), (0, -1), (-1, 1), (-1, -1)]
 
     def exists(vb, vg):
@@ -233,22 +246,31 @@
             jnp.logical_and(g + vg >= 0, g + vg < groups),
         )
 
-    def greet(vb, vg):
+    def greet(semaphore, vb, vg):
         pl.semaphore_signal(
-            barrier, inc=1, device_id=(vb, vg), device_id_type=pl.DeviceIdType.MESH
-        )
-
-    met = jnp.int32(bricks - 1)
-    for step in range(1, bricks):
-        greet(lax.rem(b + step, bricks), g)
-    for vb, vg in [(0, 1), (0, -1), (-1, 1), (-1, -1), (1, 1), (1, -1)]:
+            semaphore, inc=1, device_id=(vb, vg), device_id_type=pl.DeviceIdType.MESH
+        )
+
+    met = jnp.int32(0)
+    for vb, vg in steps + [(1, 0), (1, 1), (1, -1)]:
         here = exists(vb, vg)
 
         @pl.when(here)
         def _(vb=vb, vg=vg):
-            greet(b + vb, g + vg)
+            greet(barrier, b + vb, g + vg)
 
         met = met + here.astype(jnp.int32)
+
+    def spread(i):
+        for vb in (-circles[i], circles[i]):
+
+            @pl.when(exists(vb, 0))
+            def _(vb=vb):
+                greet(wider.at[i], b + vb, g)
+
+    def gather_in(i):
+        sides = [exists(vb, 0).astype(jnp.int32) for vb in (-circles[i], circles[i])]
+        pl.semaphore_wait(wider.at[i], sides[0] + sides[1])
 
     middle = pl.ds(LANES, columns)
     loads = [
@@ -273,7 +295,6 @@
         copy.start()
     for side in (0, LANES + columns):
         padded[:, :, side : side + LANES] = jnp.zeros((slices, rows, LANES), padded.dtype)
-        nxt[:, :, side : side + LANES] = jnp.zeros((1, rows, LANES), nxt.dtype)
     fill_band(band)
     for copy in fetches:
         copy.wait()
@@ -297,59 +318,76 @@
     ]
     for copy in tables:
         copy.start()
+    main, extra = pl.ds(0, slices), pl.ds(slices, 1)
+    edges = [nxt, low.at[main], high.at[main], low.at[extra], high.at[extra]]
+    for edge, (vb, vg) in zip(edges, steps):
+
+        @pl.when(jnp.logical_not(exists(-vb, -vg)))
+        def _(edge=edge):
+            edge[...] = jnp.zeros(edge.shape, edge.dtype)
+
     pl.semaphore_wait(barrier, met)
 
-    main, extra = pl.ds(0, slices), pl.ds(slices, 1)
-    plan = [
-        (vol.at[pl.ds(0, 1)], nxt.at[:, :, middle]),
-        (last, low.at[main]),
-        (first, high.at[main]),
-        (last.at[pl.ds(0, 1)], low.at[extra]),
-        (first.at[pl.ds(0, 1)], high.at[extra]),
-    ]
-
-    def halo(i):
-        (vb, vg), (source, target) = steps[i], plan[i]
+    blocks = bricks // QUARTERS
+    wide = columns // QUARTERS
+
+    def halo(i, turn):
+        (vb, vg) = steps[i]
+        return lambda receiver: halo_copy(i, vb, vg, flipped(receiver // blocks, turn, QUARTERS))
+
+    def halo_copy(i, vb, vg, quarter):
+        some = pl.ds(pl.multiple_of(quarter * wide, LANES), wide)
+        start = pl.multiple_of(quarter * wide, LANES)
+        source, target = [
+            (padded.at[pl.ds(0, 1), :, pl.ds(start, wide + 2 * LANES)], nxt.at[pl.ds(quarter, 1)]),
+            (last.at[:, :, some], low.at[main, :, some]),
+            (first.at[:, :, some], high.at[main, :, some]),
+            (last.at[pl.ds(0, 1), :, some], low.at[extra, :, some]),
+            (first.at[pl.ds(0, 1), :, some], high.at[extra, :, some]),
+        ][i]
         return pltpu.make_async_remote_copy(
             src_ref=source,
             dst_ref=target,
-            send_sem=send.at[i],
-            recv_sem=recv.at[i],
+            send_sem=send.at[i, quarter],
+            recv_sem=recv.at[i, quarter],
             device_id=(b + vb, g + vg),
             device_id_type=pl.DeviceIdType.MESH,
         )
 
-    for i, (vb, vg) in enumerate(steps):
-
-        @pl.when(exists(vb, vg))
-        def _(i=i):
-            halo(i).start()
-
-        @pl.when(jnp.logical_not(exists(-vb, -vg)))
-        def _(i=i):
-            plan[i][1][...] = jnp.zeros(plan[i][1].shape, plan[i][1].dtype)
+    def start_halo(count, carry):
+        for i, (vb, vg) in enumerate(steps):
+
+            @pl.when(exists(vb, vg))
+            def _(i=i, vb=vb):
+                halo(i, QUARTERS - 1 - count)(b + vb).start()
+
+        return carry
+
+    def await_halo(turn):
+        for i, (vb, vg) in enumerate(steps):
+
+            @pl.when(exists(-vb, -vg))
+            def _(i=i):
+                halo(i, turn)(b).wait_recv()
 
     def ready(tile, carry):
-        for at in range(0, slices, slices):
-            prepare(tile, slices + 1, padded, at, slices, at, band, vals, grads)
+        prepare(tile, slices + 1, padded, 0, slices, 0, 0, band, vals, grads, squares)
         return carry
 
-    lax.fori_loop(0, tiles, ready, 0)
-
-    for i, (vb, vg) in enumerate(steps):
-
-        @pl.when(exists(-vb, -vg))
-        def _(i=i):
-            halo(i).wait_recv()
+    def get_ready(leg, carry):
+        start_halo(leg, 0)
+        lax.fori_loop(leg * around, (leg + 1) * around, ready, 0)
+        return carry
+
+    around = tiles // QUARTERS
+    for i in range(len(circles)):
+        spread(i)
+        lax.fori_loop(i, i + 1 if i + 1 < len(circles) else QUARTERS, get_ready, 0)
+        if i + 1 < len(circles):
+            gather_in(i)
 
     for copy in tables:
         copy.wait()
-
-    def ready_next(tile, carry):
-        prepare(tile, slices + 1, nxt, slices, 1, 0, band, vals, grads)
-        return carry
-
-    lax.fori_loop(0, tiles, ready_next, 0)
 
     scales = [2.0 * LIMIT / bound for bound in bounds]
 
@@ -375,14 +413,31 @@
 
     half = 0.5 * (bins - 1)
 
-    def closed(tile, carry):
-        close_edges(tile, low, high, vals, grads)
-        return carry
-
-    lax.fori_loop(0, tiles, closed, 0)
+    def close(tile):
+        quarter = tile // around
+        prepare(
+            tile, slices + 1, nxt, slices, 1, quarter, quarter * around, band, vals, grads, squares
+        )
+        close_edges(tile, low, high, vals, grads, squares)
+
+    await_halo(QUARTERS - 1)
+    for i in range(AHEAD):
+        close(tile_of(i))
     levels(tile_of(0), 0, places, parts, vals, grads, half, cells, weights, shades)
 
     def march(i, carry):
+        @pl.when(i == 1)
+        def _():
+            gather_in(len(circles) - 1)
+
+        @pl.when(jnp.logical_and(i >= 1, i <= (bricks - 1) * per))
+        def _():
+            give_away(i - 1).start()
+
+        @pl.when(jnp.logical_and((i + AHEAD) % around == 0, i + AHEAD < tiles))
+        def _():
+            await_halo(QUARTERS - 1 - (i + AHEAD) // around)
+
         tile = tile_of(i)
         zero = jnp.zeros((STRIP, LANES), jnp.float32)
         state = [(zero + 1.0, zero, zero, [zero] * 3) for _ in range(rows // STRIP)]
@@ -392,6 +447,7 @@
             state = composite(tile, number, rates, pairs, cells, weights, shades, state)
         after = tile_of(jnp.minimum(i + 1, tiles - 1))
         levels(after, 0, places, parts, vals, grads, half, cells, weights, shades)
+        close(tile_of(jnp.minimum(i + AHEAD, tiles - 1)))
         result = []
         for c in range(3):
             paint = [paint[c] + nears + fars * (1.0 / LEVEL) for _, nears, fars, paint in state]
@@ -401,10 +457,6 @@
             code = (value * scales[c] + 0.5).astype(jnp.int32) - LIMIT
             mine[tile, c] = code.astype(jnp.int16)
 
-        @pl.when(jnp.logical_and(i >= 1, i <= (bricks - 1) * per))
-        def _():
-            give_away(i - 1).start()
-
         return carry
 
     lax.fori_loop(0, tiles, march, 0)
@@ -414,8 +466,9 @@
     for i, (vb, vg) in enumerate(steps):
 
         @pl.when(exists(vb, vg))
-        def _(i=i):
-            halo(i).wait_send()
+        def _(i=i, vb=vb):
+            for turn in range(QUARTERS):
+                halo(i, turn)(b + vb).wait_send()
 
     for i in range((bricks - 1) * per):
         give_away(i).wait()
@@ -459,7 +512,7 @@
             pltpu.VMEM((MOST, LANES), jnp.int32),
             pltpu.VMEM((2, MOST, LANES), jnp.float32),
             pltpu.VMEM((slices, rows, columns + 2 * LANES), volume.dtype),
-            pltpu.VMEM((1, rows, columns + 2 * LANES), volume.dtype),
+            pltpu.VMEM((QUARTERS, rows, columns // QUARTERS + 2 * LANES), volume.dtype),
             pltpu.VMEM((slices + 1, 1, columns), jnp.float32),
             pltpu.VMEM((slices + 1, 1, columns), jnp.float32),
             pltpu.VMEM((slices, 1, columns), jnp.float32),
@@ -467,6 +520,7 @@
             pltpu.VMEM((3 * LANES, LANES), jnp.bfloat16),
             pltpu.VMEM((tiles * (slices + 1), rows + 2 * PAD, LANES), jnp.float32),
             pltpu.VMEM((tiles * (slices + 1), rows, LANES), jnp.float32),
+            pltpu.VMEM((tiles * (slices + 1), 2 * STRIP, LANES), jnp.float32),
             pltpu.VMEM((ROUNDS, GROUP * (rows // STRIP), STRIP, LANES), jnp.int32),
             pltpu.VMEM((ROUNDS, GROUP * (rows // STRIP), 2 * STRIP, LANES), jnp.bfloat16),
             pltpu.VMEM((ROUNDS, GROUP * (rows // STRIP), STRIP, LANES), jnp.float32),
@@ -474,10 +528,11 @@
             pltpu.VMEM((bricks, per, 4, rows, LANES), jnp.int16),
             pltpu.SemaphoreType.DMA((8,)),
             pltpu.SemaphoreType.DMA((slices // CHUNK,)),
-            pltpu.SemaphoreType.DMA((5,)),
-            pltpu.SemaphoreType.DMA((5,)),
+            pltpu.SemaphoreType.DMA((5, QUARTERS)),
+            pltpu.SemaphoreType.DMA((5, QUARTERS)),
             pltpu.SemaphoreType.DMA((bricks, per)),
             pltpu.SemaphoreType.DMA((bricks, per)),
+            pltpu.SemaphoreType.REGULAR((len(spread_circles(bricks)),)),
         ],
         compiler_params=pltpu.CompilerParams(
             collective_id=0, has_side_effects=True, vmem_limit_bytes=GRANT

time: 33.2 us -> 29.4 us (0.89)
  Pallas kernels: 31.5 us -> 27.6 us
    pallas_call x1, Pallas kernels: 31.5 us -> 27.6 us  [shards(): pl.pallas_call(functools.partial(render_kernel, bricks, groups), out_shap...]
where the time goes in v3:
time: 29.4 us; the launch traced here: 29.2 us
  Pallas kernels  27.6 us (94%)
  local copies, waits for them, and re-layouts  1.57 us (5%)
    pallas_call x1, Pallas kernels, shards(): pl.pallas_call(functools.partial(render_kernel, bricks, groups), out_shap...  27.6 us
    unnamed x1, local copies, waits for them, and re-layouts  1.57 us

profile of v3, /device:TPU:0, one launch (start us, length us, event | category | flops | bytes accessed | tf_op | source)
XLA Modules:
  0.0 29.2 jit_solution(12584475923748607929)
XLA Ops:
  0.0 27.6 %render.1 = f32[4,32,256]{2,1,0:T(8,128)} custom-call(s32[1,1,16]{2,1,0:T(1,128)} %listed_in.1, s32[1,1,16]{2,1,0:T(1,128)} %counts_in.1, s32[8]{0:T(128)} %order_in.1, bf16[16,32,2048]{2,1,0:T(8,128)(2,1)} %vol.1, bf16[3,128]{1,0:T(4,128)(2,1)} %colors_in.1, bf16[1,128]{1,0:T(2,128)(2,1)} %bitcast.1), custom_call_target="tpu_custom_call" | custom-call | tf_op jit(solution)/shard_map/render/pallas_call | solution.py:498
  27.7 1.6 %copy.8 = f32[4,32,256]{2,1,0:T(8,128)} copy(f32[4,32,256]{2,1,0:T(8,128)} %render.1) | data formatting | bytes 262144

commit v4 on v3

--- a/solution.py
+++ b/solution.py
@@ -48,7 +48,7 @@
 
 
 def spread_circles(bricks):
-    known, circles = 1, []
+    known, circles = 2, []
     while known < bricks - 1:
         circles.append(known)
         known += known
@@ -64,11 +64,10 @@
 
 
 def lookup_tables(colors, density):
-    entries = [colors[c : c + 1, :] * LEVEL - 1.0 for c in range(3)] + [density * FINE]
     pairs = []
-    for entry in entries:
+    for entry, low in [(colors[c : c + 1, :] * LEVEL, 1.0) for c in range(3)] + [(density * FINE, 0.0)]:
         here = jnp.broadcast_to(entry, (STRIP, LANES))
-        pairs.append(here + pltpu.roll(here, LANES - 1, 1) * (1.0 / LEVEL))
+        pairs.append((here - low) + pltpu.roll(here, LANES - 1, 1) * (1.0 / LEVEL))
     return pairs
 
 
@@ -99,35 +98,36 @@
     ).astype(band.dtype)
 
 
-def along_squares(padded, at, count, tile, band):
+def prepare(tile, many, depth, padded, first, count, at, shift, band, vals, grads, squares):
     rows = padded.shape[1]
     blocks = [
         padded[
-            pl.ds(at, count), :, pl.ds(pl.multiple_of((tile + i) * LANES, LANES), LANES)
+            pl.ds(at, count), :, pl.ds(pl.multiple_of((tile - shift + i) * LANES, LANES), LANES)
         ].reshape(count * rows, LANES)
-        for i in range(3)
+        for i in range(many + 2)
     ]
     along = jnp.dot(
-        jnp.concatenate(blocks, axis=1), band[...], preferred_element_type=jnp.float32
-    ).reshape(count, rows, LANES)
-    return along * along, blocks[1].astype(jnp.float32).reshape(count, rows, LANES)
-
-
-def prepare(tile, depth, padded, first, count, at, shift, band, vals, grads, squares):
-    rows = padded.shape[1]
-    square, mid = along_squares(padded, at, count, tile - shift, band)
-    for j in range(count):
-        vals[tile * depth + first + j, PAD : PAD + rows, :] = mid[j] * 0.5
-    inner = slice(STRIP, rows - STRIP)
-    for j in range(count):
-        z = first + j
-        across = (
-            vals[tile * depth + z, PAD + STRIP + 1 : PAD + rows - STRIP + 1, :]
-            - vals[tile * depth + z, PAD + STRIP - 1 : PAD + rows - STRIP - 1, :]
-        )
-        squares[tile * depth + z, 0:STRIP, :] = square[j, 0:STRIP]
-        grads[tile * depth + z, inner, :] = (across * across + square[j, inner]) * (1.0 / 0.6) + (1.0 / 0.6)
-        squares[tile * depth + z, STRIP : 2 * STRIP, :] = square[j, rows - STRIP : rows]
+        jnp.concatenate(blocks, axis=1),
+        band[: (many + 2) * LANES, : many * LANES],
+        preferred_element_type=jnp.float32,
+    )
+    base = tile * depth + first
+    for one in range(many):
+        square = along[:, one * LANES : (one + 1) * LANES].reshape(count, rows, LANES)
+        square = square * square
+        mid = blocks[one + 1].astype(jnp.float32).reshape(count, rows, LANES)
+        for j in range(count):
+            vals[base + one * depth + j, PAD : PAD + rows, :] = mid[j] * 0.5
+        inner = slice(STRIP, rows - STRIP)
+        for j in range(count):
+            row = base + one * depth + j
+            across = (
+                vals[row, PAD + STRIP + 1 : PAD + rows - STRIP + 1, :]
+                - vals[row, PAD + STRIP - 1 : PAD + rows - STRIP - 1, :]
+            )
+            squares[row, 0:STRIP, :] = square[j, 0:STRIP]
+            grads[row, inner, :] = (across * across + square[j, inner]) * (1.0 / 0.6) + (1.0 / 0.6)
+            squares[row, STRIP : 2 * STRIP, :] = square[j, rows - STRIP : rows]
 
 
 def close_edges(tile, low, high, vals, grads, squares):
@@ -171,12 +171,12 @@
         rate = rates[number * GROUP + inner, tile]
         for strip in range(strips):
             unit = inner * strips + strip
-            remain, nears, fars, paint = carry[strip]
+            remain, fars, paint = carry[strip]
             index = cells[number, unit]
             both = weights[number, unit].astype(jnp.float32)
             upper, lower = both[:STRIP] * LEVEL, both[STRIP:]
             found = [gather_lanes(pair, index) for pair in pairs]
-            whole = [jnp.floor(value) for value in found]
+            whole = [jnp.ceil(value) for value in found[:3]] + [jnp.floor(found[3])]
             after = [value - first for value, first in zip(found, whole)]
             sigma = lower * whole[3] + upper * after[3]
             left = remain * jnp.exp2(sigma * rate)
@@ -184,7 +184,7 @@
             near = weight * lower
             far = weight * upper
             paint = [paint[c] + near * whole[c] + far * after[c] for c in range(3)]
-            carry[strip] = (left, nears + near, fars + far, paint)
+            carry[strip] = (left, fars + far, paint)
     return carry
 
 
@@ -193,14 +193,12 @@
     groups,
     listed_in,
     counts_in,
-    order_in,
     vol,
     colors_in,
     density_in,
-    out,
+    held,
     listed,
     counts,
-    order,
     places,
     parts,
     rates,
@@ -222,13 +220,13 @@
     weights,
     shades,
     mine,
-    held,
     small,
     load,
     send,
     recv,
     give,
     take,
+    keep,
     wider,
 ):
     b, g = lax.axis_index("view"), lax.axis_index("img")
@@ -252,7 +250,7 @@
         )
 
     met = jnp.int32(0)
-    for vb, vg in steps + [(1, 0), (1, 1), (1, -1)]:
+    for vb, vg in steps + [(1, 0), (1, 1), (1, -1), (2, 0), (-2, 0)]:
         here = exists(vb, vg)
 
         @pl.when(here)
@@ -287,7 +285,6 @@
                 (density_in, density_ref),
                 (counts_in, counts),
                 (listed_in, listed),
-                (order_in, order),
             ]
         )
     ]
@@ -355,11 +352,12 @@
         )
 
     def start_halo(count, carry):
-        for i, (vb, vg) in enumerate(steps):
+        turn = QUARTERS - 1 - count
+        for i, (vb, vg) in reversed(list(enumerate(steps))):
 
             @pl.when(exists(vb, vg))
             def _(i=i, vb=vb):
-                halo(i, QUARTERS - 1 - count)(b + vb).start()
+                halo(i, turn)(b + vb).start()
 
         return carry
 
@@ -371,20 +369,21 @@
                 halo(i, turn)(b).wait_recv()
 
     def ready(tile, carry):
-        prepare(tile, slices + 1, padded, 0, slices, 0, 0, band, vals, grads, squares)
+        prepare(tile * 2, 2, slices + 1, padded, 0, slices, 0, 0, band, vals, grads, squares)
         return carry
 
     def get_ready(leg, carry):
         start_halo(leg, 0)
-        lax.fori_loop(leg * around, (leg + 1) * around, ready, 0)
+        lax.fori_loop(leg * (around // 2), (leg + 1) * (around // 2), ready, 0)
         return carry
 
     around = tiles // QUARTERS
-    for i in range(len(circles)):
+    spread(0)
+    lax.fori_loop(0, QUARTERS - 1, get_ready, 0)
+    for i in range(1, len(circles)):
+        gather_in(i - 1)
         spread(i)
-        lax.fori_loop(i, i + 1 if i + 1 < len(circles) else QUARTERS, get_ready, 0)
-        if i + 1 < len(circles):
-            gather_in(i)
+    lax.fori_loop(QUARTERS - 1, QUARTERS, get_ready, 0)
 
     for copy in tables:
         copy.wait()
@@ -392,7 +391,8 @@
     scales = [2.0 * LIMIT / bound for bound in bounds]
 
     def place(i):
-        mask, part = bricks - 1 - i // per, i % per
+        turn = i
+        mask, part = bricks - 1 - turn // per, turn % per
         peer = flipped(b, mask, bricks)
         return mask, part, peer
 
@@ -416,7 +416,7 @@
     def close(tile):
         quarter = tile // around
         prepare(
-            tile, slices + 1, nxt, slices, 1, quarter, quarter * around, band, vals, grads, squares
+            tile, 1, slices + 1, nxt, slices, 1, quarter, quarter * around, band, vals, grads, squares
         )
         close_edges(tile, low, high, vals, grads, squares)
 
@@ -434,13 +434,15 @@
         def _():
             give_away(i - 1).start()
 
-        @pl.when(jnp.logical_and((i + AHEAD) % around == 0, i + AHEAD < tiles))
-        def _():
-            await_halo(QUARTERS - 1 - (i + AHEAD) // around)
+        for first_use, turn in ((around, 2), (2 * around, 1), (3 * around, 0)):
+
+            @pl.when(i + AHEAD == first_use)
+            def _(turn=turn):
+                await_halo(turn)
 
         tile = tile_of(i)
         zero = jnp.zeros((STRIP, LANES), jnp.float32)
-        state = [(zero + 1.0, zero, zero, [zero] * 3) for _ in range(rows // STRIP)]
+        state = [(zero + 1.0, zero, [zero] * 3) for _ in range(rows // STRIP)]
         for number in range(ROUNDS):
             if number + 1 < ROUNDS:
                 levels(tile, number + 1, places, parts, vals, grads, half, cells, weights, shades)
@@ -450,7 +452,7 @@
         close(tile_of(jnp.minimum(i + AHEAD, tiles - 1)))
         result = []
         for c in range(3):
-            paint = [paint[c] + nears + fars * (1.0 / LEVEL) for _, nears, fars, paint in state]
+            paint = [paint[c] + fars for _, fars, paint in state]
             result.append(jnp.concatenate(paint, axis=0) * (1.0 / LEVEL))
         result.append(1.0 - jnp.concatenate([remain for remain, *_ in state], axis=0))
         for c, value in enumerate(result):
@@ -460,9 +462,12 @@
         return carry
 
     lax.fori_loop(0, tiles, march, 0)
-    for part in range(per):
-        held[b, part] = mine[b * per + part]
-    units = [jnp.broadcast_to(bound / (2.0 * LIMIT), (rows, LANES)) for bound in bounds]
+    own = [
+        pltpu.make_async_copy(mine.at[b * per + part], held.at[b, part], keep.at[part])
+        for part in range(per)
+    ]
+    for copy in own:
+        copy.start()
     for i, (vb, vg) in enumerate(steps):
 
         @pl.when(exists(vb, vg))
@@ -470,10 +475,36 @@
             for turn in range(QUARTERS):
                 halo(i, turn)(b + vb).wait_send()
 
+    for copy in own:
+        copy.wait()
     for i in range((bricks - 1) * per):
         give_away(i).wait()
 
+
+def blend_kernel(
+    slices, order_in, held_in, colors_in, density_in, out, order, held, colors, density, done, load, save
+):
+    bricks, per, _, rows, _ = held.shape
+    smalls = [(order_in, order), (colors_in, colors), (density_in, density)]
+    smalls = [
+        pltpu.make_async_copy(source, target, load.at[per + i])
+        for i, (source, target) in enumerate(smalls)
+    ]
+    loads = [
+        pltpu.make_async_copy(held_in.at[:, part], held.at[:, part], load.at[part])
+        for part in range(per)
+    ]
+    for copy in smalls + loads:
+        copy.start()
+    for copy in smalls:
+        copy.wait()
+    bounds = channel_bounds(
+        colors[...].astype(jnp.float32), density[...].astype(jnp.float32), slices
+    )
+    units = [jnp.broadcast_to(bound / (2.0 * LIMIT), (rows, LANES)) for bound in bounds]
+    saves = []
     for part in range(per):
+        loads[part].wait()
         image = [jnp.zeros((rows, LANES), jnp.float32) for _ in range(4)]
         remain = jnp.ones((rows, LANES), jnp.float32)
         for position in range(bricks):
@@ -485,7 +516,15 @@
             image = [image[c] + remain * value[c] for c in range(4)]
             remain = remain * (1.0 - value[3])
         for c in range(4):
-            out[c, :, part * LANES : (part + 1) * LANES] = image[c]
+            done[part, c] = image[c]
+        saves.append(
+            pltpu.make_async_copy(
+                done.at[part], out.at[:, :, part * LANES : (part + 1) * LANES], save.at[part]
+            )
+        )
+        saves[-1].start()
+    for copy in saves:
+        copy.wait()
 
 
 def shards(volume, occupied, sample_counts, depth_order, colors, density):
@@ -493,17 +532,15 @@
     bricks, groups = lax.axis_size("view"), lax.axis_size("img")
     tiles = columns // LANES
     per = tiles // bricks
-    vmem = pl.BlockSpec(memory_space=pltpu.VMEM)
     hbm = pl.BlockSpec(memory_space=pltpu.HBM)
-    return pl.pallas_call(
+    held = pl.pallas_call(
         functools.partial(render_kernel, bricks, groups),
-        out_shape=jax.ShapeDtypeStruct((4, rows, per * LANES), jnp.float32),
-        in_specs=[hbm] * 6,
-        out_specs=vmem,
+        out_shape=jax.ShapeDtypeStruct((bricks, per, 4, rows, LANES), jnp.int16),
+        in_specs=[hbm] * 5,
+        out_specs=hbm,
         scratch_shapes=[
             pltpu.SMEM(occupied.shape, jnp.int32),
             pltpu.SMEM(sample_counts.shape, jnp.int32),
-            pltpu.SMEM(depth_order.shape, jnp.int32),
             pltpu.SMEM((MOST, LANES), jnp.int32),
             pltpu.SMEM((MOST, LANES), jnp.float32),
             pltpu.SMEM((MOST, LANES), jnp.float32),
@@ -517,7 +554,7 @@
             pltpu.VMEM((slices + 1, 1, columns), jnp.float32),
             pltpu.VMEM((slices, 1, columns), jnp.float32),
             pltpu.VMEM((slices, 1, columns), jnp.float32),
-            pltpu.VMEM((3 * LANES, LANES), jnp.bfloat16),
+            pltpu.VMEM((4 * LANES, 2 * LANES), jnp.bfloat16),
             pltpu.VMEM((tiles * (slices + 1), rows + 2 * PAD, LANES), jnp.float32),
             pltpu.VMEM((tiles * (slices + 1), rows, LANES), jnp.float32),
             pltpu.VMEM((tiles * (slices + 1), 2 * STRIP, LANES), jnp.float32),
@@ -525,20 +562,37 @@
             pltpu.VMEM((ROUNDS, GROUP * (rows // STRIP), 2 * STRIP, LANES), jnp.bfloat16),
             pltpu.VMEM((ROUNDS, GROUP * (rows // STRIP), STRIP, LANES), jnp.float32),
             pltpu.VMEM((tiles, 4, rows, LANES), jnp.int16),
-            pltpu.VMEM((bricks, per, 4, rows, LANES), jnp.int16),
             pltpu.SemaphoreType.DMA((8,)),
             pltpu.SemaphoreType.DMA((slices // CHUNK,)),
             pltpu.SemaphoreType.DMA((5, QUARTERS)),
             pltpu.SemaphoreType.DMA((5, QUARTERS)),
             pltpu.SemaphoreType.DMA((bricks, per)),
             pltpu.SemaphoreType.DMA((bricks, per)),
+            pltpu.SemaphoreType.DMA((per,)),
             pltpu.SemaphoreType.REGULAR((len(spread_circles(bricks)),)),
         ],
         compiler_params=pltpu.CompilerParams(
             collective_id=0, has_side_effects=True, vmem_limit_bytes=GRANT
         ),
         name="render",
-    )(occupied, sample_counts, depth_order, volume, colors, density[None, :])
+    )(occupied, sample_counts, volume, colors, density[None, :])
+    return pl.pallas_call(
+        functools.partial(blend_kernel, slices),
+        out_shape=jax.ShapeDtypeStruct((4, rows, per * LANES), jnp.float32),
+        in_specs=[hbm] * 4,
+        out_specs=hbm,
+        scratch_shapes=[
+            pltpu.SMEM(depth_order.shape, jnp.int32),
+            pltpu.VMEM(held.shape, held.dtype),
+            pltpu.VMEM(colors.shape, colors.dtype),
+            pltpu.VMEM((1, density.shape[0]), density.dtype),
+            pltpu.VMEM((per, 4, rows, LANES), jnp.float32),
+            pltpu.SemaphoreType.DMA((per + 3,)),
+            pltpu.SemaphoreType.DMA((per,)),
+        ],
+        compiler_params=pltpu.CompilerParams(vmem_limit_bytes=GRANT),
+        name="blend",
+    )(depth_order, held, colors, density[None, :])
 
 
 def solution(mesh):

time: 29.4 us -> 27.9 us (0.949)
  local copies, waits for them, and re-layouts: 1.57 us -> 0 us
    pallas_call x0 -> x1, Pallas kernels: none -> 1.9 us  [shards(): pl.pallas_call(functools.partial(blend_kernel, slices), out_shape=jax.Sha...]
    pallas_call x1, Pallas kernels: 27.6 us -> 25.8 us  [shards(): pl.pallas_call(functools.partial(render_kernel, bricks, groups), out_shap...]
    unnamed x1 -> x0, local copies, waits for them, and re-layouts: 1.57 us -> none
where the time goes in v4:
time: 27.9 us; the launch traced here: 27.7 us
  Pallas kernels  27.7 us (99%)
    pallas_call x1, Pallas kernels, shards(): pl.pallas_call(functools.partial(render_kernel, bricks, groups), out_shap...  25.8 us
    pallas_call x1, Pallas kernels, shards(): pl.pallas_call(functools.partial(blend_kernel, slices), out_shape=jax.Sha...  1.9 us

profile of v4, /device:TPU:0, one launch (start us, length us, event | category | flops | bytes accessed | tf_op | source)
XLA Modules:
  0.0 27.7 jit_solution(141758656369905976)
XLA Ops:
  0.0 25.8 %render.1.held_in = s16[8,2,4,32,128]{4,3,2,1,0:T(8,128)(2,1)} custom-call(s32[1,1,16]{2,1,0:T(1,128)} %listed_in.1, s32[1,1,16]{2,1,0:T(1,128)} %counts_in.1, bf16[16,32,2048]{2,1,0:T(8,128)(2,1)} %vol.1, bf16[3,128]{1,0:T(4,128)(2,1)} %colors_in.3, bf16[1,128]{1,0:T(2,128)(2,1)} %bitcast.1), custom_call_target="tpu_custom_call" | custom-call | tf_op jit(solution)/shard_map/render/pallas_call | solution.py:536
  25.8 1.9 %blend.1 = f32[4,32,256]{2,1,0:T(8,128)} custom-call(s32[8]{0:T(128)} %order_in.1, s16[8,2,4,32,128]{4,3,2,1,0:T(8,128)(2,1)} %render.1.held_in, bf16[3,128]{1,0:T(4,128)(2,1)} %colors_in.3, bf16[1,128]{1,0:T(2,128)(2,1)} %bitcast.2), custom_call_target="tpu_custom_call" | custom-call | tf_op jit(solution)/shard_map/blend/pallas_call | solution.py:579

commit v5 on v4

--- a/solution.py
+++ b/solution.py
@@ -388,7 +388,7 @@
     for copy in tables:
         copy.wait()
 
-    scales = [2.0 * LIMIT / bound for bound in bounds]
+    scales = [2.0 * LIMIT / bound / (LEVEL if c < 3 else 1.0) for c, bound in enumerate(bounds)]
 
     def place(i):
         turn = i
@@ -434,7 +434,7 @@
         def _():
             give_away(i - 1).start()
 
-        for first_use, turn in ((around, 2), (2 * around, 1), (3 * around, 0)):
+        for first_use, turn in [((QUARTERS - 1 - turn) * around, turn) for turn in range(QUARTERS - 1)]:
 
             @pl.when(i + AHEAD == first_use)
             def _(turn=turn):
@@ -453,7 +453,7 @@
         result = []
         for c in range(3):
             paint = [paint[c] + fars for _, fars, paint in state]
-            result.append(jnp.concatenate(paint, axis=0) * (1.0 / LEVEL))
+            result.append(jnp.concatenate(paint, axis=0))
         result.append(1.0 - jnp.concatenate([remain for remain, *_ in state], axis=0))
         for c, value in enumerate(result):
             code = (value * scales[c] + 0.5).astype(jnp.int32) - LIMIT

time: 27.9 us -> 27.8 us (level)
  no operation moved by 1% of the time
where the time goes in v5:
time: 27.8 us; the launch traced here: 27.6 us
  Pallas kernels  27.6 us (99%)
    pallas_call x1, Pallas kernels, shards(): pl.pallas_call(functools.partial(render_kernel, bricks, groups), out_shap...  25.7 us
    pallas_call x1, Pallas kernels, shards(): pl.pallas_call(functools.partial(blend_kernel, slices), out_shape=jax.Sha...  1.9 us

profile of v5, /device:TPU:0, one launch (start us, length us, event | category | flops | bytes accessed | tf_op | source)
XLA Modules:
  0.0 27.6 jit_solution(5163629151144466681)
XLA Ops:
  0.0 25.7 %render.1.held_in = s16[8,2,4,32,128]{4,3,2,1,0:T(8,128)(2,1)} custom-call(s32[1,1,16]{2,1,0:T(1,128)} %listed_in.1, s32[1,1,16]{2,1,0:T(1,128)} %counts_in.1, bf16[16,32,2048]{2,1,0:T(8,128)(2,1)} %vol.1, bf16[3,128]{1,0:T(4,128)(2,1)} %colors_in.3, bf16[1,128]{1,0:T(2,128)(2,1)} %bitcast.1), custom_call_target="tpu_custom_call" | custom-call | tf_op jit(solution)/shard_map/render/pallas_call | solution.py:536
  25.7 1.9 %blend.1 = f32[4,32,256]{2,1,0:T(8,128)} custom-call(s32[8]{0:T(128)} %order_in.1, s16[8,2,4,32,128]{4,3,2,1,0:T(8,128)(2,1)} %render.1.held_in, bf16[3,128]{1,0:T(4,128)(2,1)} %colors_in.3, bf16[1,128]{1,0:T(2,128)(2,1)} %bitcast.2), custom_call_target="tpu_custom_call" | custom-call | tf_op jit(solution)/shard_map/blend/pallas_call | solution.py:579
